TPU v7x, 32 devices: a whole 2x2x4 slice. The times are simulated.
32 devices in a mesh: wide: 8 (over z, x), narrow: 4 (over y, core).
Axes of the slice: x: 2, y: 2, z: 4, core: 2. Of those that a mesh axis runs over, the one named last changes fastest.
Arguments:
- tokens: bfloat16 [20480, 1024], P(('wide', 'narrow')), may hold values from -6 to 6
- cotangent: bfloat16 [20480, 1024], P(('wide', 'narrow')), may hold values from -6 to 6
- flags: int32 [8], P('wide'), may hold values from 0 to 1
- norm_gain: bfloat16 [1024], replicated, may hold values from 0.5 to 1.5
- query_weight: bfloat16 [1024, 512], P(None, 'narrow'), may hold values from -0.1875 to 0.1875
- key_weight: bfloat16 [1024, 512], P(None, 'narrow'), may hold values from -0.1875 to 0.1875
- value_weight: bfloat16 [1024, 1024], P(None, 'narrow'), may hold values from -0.1875 to 0.1875
- swish_weight: bfloat16 [1024, 1024], P(None, 'narrow'), may hold values from -0.1875 to 0.1875
- rank_down: bfloat16 [1024, 16], replicated, may hold values from -0.1875 to 0.1875
- rank_up: bfloat16 [16, 512], replicated, may hold values from -0.375 to 0.375
- decay_bias: bfloat16 [512], replicated, may hold values from 0 to 10
- group_gain: bfloat16 [256], replicated, may hold values from 0.5 to 1.5
- output_weight: bfloat16 [1024, 1024], P('narrow'), may hold values from -0.1875 to 0.1875
- mlp_gain: bfloat16 [1024], replicated, may hold values from 0.5 to 1.5
- mlp_gate: bfloat16 [1024, 2816], P(None, 'narrow'), may hold values from -0.1875 to 0.1875
- mlp_up: bfloat16 [1024, 2816], P(None, 'narrow'), may hold values from -0.1875 to 0.1875
- mlp_down: bfloat16 [2816, 1024], P('narrow'), may hold values from -0.109375 to 0.109375
Outputs:
- result: bfloat16 [20480, 1024], P(('wide', 'narrow'))
- input_grad: float32 [20480, 1024], P(('wide', 'narrow'))
- norm_gain_grad: float32 [1024], replicated
- query_grad: float32 [1024, 512], P('wide', 'narrow')
- key_grad: float32 [1024, 512], P('wide', 'narrow')
- value_grad: float32 [1024, 1024], P('wide', 'narrow')
- swish_grad: float32 [1024, 1024], P('wide', 'narrow')
- rank_down_grad: float32 [1024, 16], replicated
- rank_up_grad: float32 [16, 512], replicated
- decay_bias_grad: float32 [512], replicated
- group_gain_grad: float32 [256], replicated
- output_grad: float32 [1024, 1024], P('narrow', 'wide')
- mlp_gain_grad: float32 [1024], replicated
- mlp_gate_grad: float32 [1024, 2816], P('wide', 'narrow')
- mlp_up_grad: float32 [1024, 2816], P('wide', 'narrow')
- mlp_down_grad: float32 [2816, 1024], P('narrow', 'wide')
All inputs are finite; a program needn't handle non-finite values.
Results may differ from a plain program's by a relative error of at most 0.03.
Values may be sent and summed in bfloat16 or wider, within the bound.
A program may use at most 192 MiB of HBM per device.

v0:
```python
import jax
import jax.numpy as jnp
from jax import lax
from jax.sharding import PartitionSpec as P

SPAN = 64


NORM_EPS = 1e-06
GROUP_EPS = 1e-05
GATE_NORM = 16.0
HIGHEST_PREC = lax.Precision.HIGHEST


def prefix_2(array, axis, combine, identity):
    count, place = (lax.axis_size(axis), lax.axis_index(axis))
    everything = jax.tree.map(
        lambda part, kind: lax.all_gather(part.astype(kind), axis),
        array,
        (jnp.bfloat16, jnp.bfloat16),
    )
    start = jax.tree.map(
        lambda part, zero: jnp.broadcast_to(jnp.asarray(zero, part.dtype), part.shape),
        array,
        identity,
    )

    def hop(k, before):
        reached = k < place
        new = combine(
            before, jax.tree.map(lambda part, own: part[k].astype(own.dtype), everything, array)
        )
        return jax.tree.map(lambda a, b: jnp.where(reached, a, b), new, before)

    return lax.fori_loop(0, count, hop, start)


def prefix_3(array, axis, join, neutral):
    count = lax.axis_size(axis)
    place = lax.axis_index(axis)
    ahead = count - 1 - place
    gathered = jax.tree.map(
        lambda a, kind: lax.all_gather(a.astype(kind), axis),
        array,
        jax.tree.map(lambda a: jnp.bfloat16 if a.dtype == jnp.float32 else a.dtype, array),
    )
    state = jax.tree.map(lambda a, e: jnp.zeros_like(a) + jnp.asarray(e, a.dtype), array, neutral)

    def one(hop, state):
        source = count - 1 - hop
        return join(
            state,
            jax.tree.map(
                lambda a, own: lax.dynamic_index_in_dim(a, source, 0, False).astype(own.dtype),
                gathered,
                array,
            ),
        )

    return lax.fori_loop(0, ahead, one, state)


def matmul(left_mat, right_mat):
    return jnp.dot(left_mat, right_mat, preferred_element_type=jnp.float32)


def matmul_tn(left_mat, right_mat):
    return lax.dot_general(
        left_mat, right_mat, (((0,), (0,)), ((), ())), preferred_element_type=jnp.float32
    )


def matmul_nt(left_mat, right_mat):
    return lax.dot_general(
        left_mat, right_mat, (((1,), (1,)), ((), ())), preferred_element_type=jnp.float32
    )


def rms_rows(values, gain_vec, eps_value):
    inv_root = lax.rsqrt(jnp.mean(values * values, axis=-1, keepdims=True) + eps_value)
    return (values * inv_root * gain_vec, inv_root)


def norm_backward(grad_normed, values, inv_root, gain_vec):
    unit_rows = values * inv_root
    weighted = grad_normed * gain_vec
    gain_part = jnp.sum(grad_normed * unit_rows, axis=0)
    grad_values = inv_root * (
        weighted - unit_rows * jnp.mean(weighted * unit_rows, axis=-1, keepdims=True)
    )
    return (grad_values, gain_part)


def segment_mix(query_rows, key_rows, value_rows, decay_rows, start_state):
    seg_len = query_rows.shape[0]
    blocks = seg_len // SPAN
    key_dim = query_rows.shape[1]
    query_blk = query_rows.reshape(blocks, SPAN, key_dim) * key_dim ** (-0.5)
    key_blk = key_rows.reshape(blocks, SPAN, key_dim)
    value_blk = value_rows.reshape(blocks, SPAN, -1)
    inner_cum = jnp.cumsum(decay_rows.reshape(blocks, SPAN, key_dim), axis=1)
    block_end = inner_cum[:, -1:, :]
    query_dec = query_blk * jnp.exp(inner_cum)
    key_dec = key_blk * jnp.exp(-inner_cum)
    key_end = key_blk * jnp.exp(block_end - inner_cum)
    causal_mask = jnp.arange(SPAN)[:, None] >= jnp.arange(SPAN)[None, :]
    scores = jnp.einsum("bik,bjk->bij", query_dec, key_dec, precision=HIGHEST_PREC)
    scores = jnp.where(causal_mask[None], scores, 0.0)
    in_block = jnp.einsum("bij,bjv->biv", scores, value_blk, precision=HIGHEST_PREC)
    block_states = jnp.einsum("bjk,bjv->bkv", key_end, value_blk, precision=HIGHEST_PREC)
    block_rates = jnp.exp(block_end[:, 0, :])

    def advance(carried, step_item):
        decay_rate, increment = step_item
        return (decay_rate[:, None] * carried + increment, carried)

    last_state, entering = lax.scan(advance, start_state, (block_rates, block_states))
    from_state = jnp.einsum("bik,bkv->biv", query_dec, entering, precision=HIGHEST_PREC)
    return ((in_block + from_state).reshape(seg_len, -1), last_state)


def segment_cumulative(decay_rows):
    seg_len, key_dim = decay_rows.shape
    blocks = seg_len // SPAN
    inner_cum = jnp.cumsum(decay_rows.reshape(blocks, SPAN, key_dim), axis=1)
    totals = inner_cum[:, -1, :]
    offsets = jnp.cumsum(totals, axis=0) - totals
    return (inner_cum + offsets[:, None, :]).reshape(seg_len, key_dim)


def compose(earlier, later_pair):
    rate_early, state_early = earlier
    rate_late, state_late = later_pair
    return (rate_early * rate_late, rate_late[:, None] * state_early + state_late)


def post_gate(mixed, swish_pre, gain_vec):
    normed_mix, _ = rms_rows(mixed, gain_vec, GROUP_EPS)
    return normed_mix * jax.nn.silu(swish_pre)


def shards(
    tokens,
    cotangent,
    flags,
    norm_gain,
    query_weight,
    key_weight,
    value_weight,
    swish_weight,
    rank_down,
    rank_up,
    decay_bias,
    group_gain,
    output_weight,
    mlp_gain,
    mlp_gate,
    mlp_up,
    mlp_down,
):
    rows_dev = tokens.shape[0]
    head_index = lax.axis_index("narrow")
    own_start = head_index * rows_dev
    key_width = query_weight.shape[1]
    value_width = value_weight.shape[1]
    rank_cols = lax.dynamic_slice_in_dim(rank_up, head_index * key_width, key_width, 1).astype(
        jnp.float32
    )
    bias_cols = lax.dynamic_slice_in_dim(decay_bias, head_index * key_width, key_width, 0).astype(
        jnp.float32
    )
    restart = 1.0 - flags[0].astype(jnp.float32)
    norm_gain_f = norm_gain.astype(jnp.float32)
    mlp_gain_f = mlp_gain.astype(jnp.float32)
    inputs = tokens.astype(jnp.float32)
    normed, inv_one = rms_rows(inputs, norm_gain_f, NORM_EPS)
    normed_all = lax.all_gather(normed.astype(jnp.bfloat16), "narrow", axis=0, tiled=True)
    query_low = matmul(normed_all, query_weight).astype(jnp.bfloat16)
    key_low = matmul(normed_all, key_weight).astype(jnp.bfloat16)
    value_low = matmul(normed_all, value_weight).astype(jnp.bfloat16)
    swish_pre = matmul(normed_all, swish_weight)
    rank_pre = matmul(normed_all, rank_down)
    decay_pre = jnp.dot(rank_pre, rank_cols, precision=HIGHEST_PREC) + bias_cols
    decay_log = jax.nn.log_sigmoid(decay_pre) / GATE_NORM
    query_f = query_low.astype(jnp.float32)
    key_f = key_low.astype(jnp.float32)
    value_f = value_low.astype(jnp.float32)
    zero_state = jnp.zeros((key_width, value_width), jnp.float32)
    base_out, local_state = segment_mix(query_f, key_f, value_f, decay_log, zero_state)
    query_reach = query_f * key_width ** (-0.5) * jnp.exp(segment_cumulative(decay_log))
    multiplier = restart * jnp.exp(jnp.sum(decay_log, axis=0))
    identity = (jnp.ones((key_width,), jnp.float32), zero_state)
    prefix = prefix_2((multiplier, local_state), "wide", compose, identity)
    enter_state = restart * prefix[1]
    mixed = base_out + jnp.dot(query_reach, enter_state, precision=HIGHEST_PREC)
    gated, post_pullback = jax.vjp(post_gate, mixed, swish_pre, group_gain.astype(jnp.float32))
    gated_low = gated.astype(jnp.bfloat16)
    full_term = matmul(gated_low, output_weight)
    own_term = lax.dynamic_slice_in_dim(full_term, own_start, rows_dev, 0) + inputs
    full_term = lax.dynamic_update_slice_in_dim(full_term, own_term, own_start, 0)
    middle_all = lax.psum(full_term.astype(jnp.bfloat16), "narrow").astype(jnp.float32)
    normed_two_all, inv_two_all = rms_rows(middle_all, mlp_gain_f, NORM_EPS)
    mlp_rows = normed_two_all.astype(jnp.bfloat16)
    middle = lax.dynamic_slice_in_dim(middle_all, own_start, rows_dev, 0)
    inv_two = lax.dynamic_slice_in_dim(inv_two_all, own_start, rows_dev, 0)
    gate_pre = matmul(mlp_rows, mlp_gate)
    up_pre = matmul(mlp_rows, mlp_up)
    gate_sig = jax.nn.sigmoid(gate_pre)
    gate_act = gate_pre * gate_sig
    hidden_low = (gate_act * up_pre).astype(jnp.bfloat16)
    result = (
        middle
        + lax.psum_scatter(
            matmul(hidden_low, mlp_down).astype(jnp.bfloat16),
            "narrow",
            scatter_dimension=0,
            tiled=True,
        ).astype(jnp.float32)
    ).astype(jnp.bfloat16)
    block_rows = lax.all_gather(cotangent, "narrow", axis=0, tiled=True)
    grad_down_t = matmul_tn(block_rows, hidden_low)
    grad_hidden = matmul_nt(block_rows, mlp_down)
    grad_down_t, grad_hidden = (grad_down_t, grad_hidden)
    grad_up_low = (grad_hidden * gate_act).astype(jnp.bfloat16)
    grad_gate_low = (grad_hidden * up_pre * gate_sig * (1.0 + gate_pre * (1.0 - gate_sig))).astype(
        jnp.bfloat16
    )
    grad_mlp_gate = matmul_tn(mlp_rows, grad_gate_low)
    grad_mlp_up = matmul_tn(mlp_rows, grad_up_low)
    grad_normed_two = lax.psum_scatter(
        (matmul_nt(grad_gate_low, mlp_gate) + matmul_nt(grad_up_low, mlp_up)).astype(jnp.bfloat16),
        "narrow",
        scatter_dimension=0,
        tiled=True,
    ).astype(jnp.float32)
    grad_middle_norm, mlp_gain_part = norm_backward(grad_normed_two, middle, inv_two, mlp_gain_f)
    grad_middle = cotangent.astype(jnp.float32) + grad_middle_norm
    middle_low = grad_middle.astype(jnp.bfloat16)
    block_rows = lax.all_gather(middle_low, "narrow", axis=0, tiled=True)
    grad_out_t = matmul_tn(block_rows, gated_low)
    grad_gated = matmul_nt(block_rows, output_weight)
    grad_out_t, grad_gated = (grad_out_t, grad_gated)
    grad_mixed, grad_swish, group_part = post_pullback(grad_gated)
    grad_swish_low = grad_swish.astype(jnp.bfloat16)
    local_back = lax.dot_general(
        query_reach, grad_mixed, (((0,), (0,)), ((), ())), precision=HIGHEST_PREC
    )
    suffix = prefix_3((multiplier, restart * local_back), "wide", compose, identity)
    _, mix_pullback = jax.vjp(segment_mix, query_f, key_f, value_f, decay_log, enter_state)
    grad_query, grad_key, grad_value, grad_decay, _ = mix_pullback((grad_mixed, suffix[1]))
    grad_query_low = grad_query.astype(jnp.bfloat16)
    grad_key_low = grad_key.astype(jnp.bfloat16)
    grad_value_low = grad_value.astype(jnp.bfloat16)
    grad_pre = grad_decay * jax.nn.sigmoid(-decay_pre) / GATE_NORM
    grad_rank_cols = lax.dot_general(
        rank_pre, grad_pre, (((0,), (0,)), ((), ())), precision=HIGHEST_PREC
    )
    grad_bias_cols = jnp.sum(grad_pre, axis=0)
    grad_rank_low = lax.dot_general(
        grad_pre, rank_cols, (((1,), (1,)), ((), ())), precision=HIGHEST_PREC
    ).astype(jnp.bfloat16)
    grad_query_w = matmul_tn(normed_all, grad_query_low)
    grad_key_w = matmul_tn(normed_all, grad_key_low)
    grad_value_w = matmul_tn(normed_all, grad_value_low)
    grad_swish_w = matmul_tn(normed_all, grad_swish_low)
    grad_rank_down = matmul_tn(normed_all, grad_rank_low)
    total = matmul_nt(grad_query_low, query_weight) + matmul_nt(grad_key_low, key_weight)
    total = total + matmul_nt(grad_value_low, value_weight)
    total = total + matmul_nt(grad_swish_low, swish_weight)
    grad_normed = lax.psum_scatter(
        (total + matmul_nt(grad_rank_low, rank_down)).astype(jnp.bfloat16),
        "narrow",
        scatter_dimension=0,
        tiled=True,
    ).astype(jnp.float32)
    grad_input_norm, norm_gain_part = norm_backward(grad_normed, inputs, inv_one, norm_gain_f)
    input_grad = grad_middle + grad_input_norm
    summed = (
        lax.psum_scatter(grad_query_w, "wide", scatter_dimension=0, tiled=True),
        lax.psum_scatter(grad_key_w, "wide", scatter_dimension=0, tiled=True),
        lax.psum_scatter(grad_value_w, "wide", scatter_dimension=0, tiled=True),
        lax.psum_scatter(grad_swish_w, "wide", scatter_dimension=0, tiled=True),
        lax.psum_scatter(grad_out_t, "wide", scatter_dimension=0, tiled=True),
        lax.psum_scatter(grad_mlp_gate, "wide", scatter_dimension=0, tiled=True),
        lax.psum_scatter(grad_mlp_up, "wide", scatter_dimension=0, tiled=True),
        lax.psum_scatter(grad_down_t, "wide", scatter_dimension=0, tiled=True),
    )
    rank_up_full = lax.dynamic_update_slice_in_dim(
        jnp.zeros(rank_up.shape, jnp.float32), grad_rank_cols, head_index * key_width, 1
    )
    bias_full = lax.dynamic_update_slice_in_dim(
        jnp.zeros(decay_bias.shape, jnp.float32), grad_bias_cols, head_index * key_width, 0
    )
    small = lax.psum(
        (norm_gain_part, mlp_gain_part, group_part, grad_rank_down, rank_up_full, bias_full),
        ("wide", "narrow"),
    )
    return (
        result,
        input_grad,
        small[0],
        summed[0],
        summed[1],
        summed[2],
        summed[3],
        small[3],
        small[4],
        small[5],
        small[2],
        summed[4].T,
        small[1],
        summed[5],
        summed[6],
        summed[7].T,
    )


def solution(mesh):
    in_specs = (
        P(("wide", "narrow"), None),
        P(("wide", "narrow"), None),
        P("wide"),
        P(),
        P(None, "narrow"),
        P(None, "narrow"),
        P(None, "narrow"),
        P(None, "narrow"),
        P(),
        P(),
        P(),
        P(),
        P("narrow", None),
        P(),
        P(None, "narrow"),
        P(None, "narrow"),
        P("narrow", None),
    )
    out_specs = (
        P(("wide", "narrow"), None),
        P(("wide", "narrow"), None),
        P(),
        P("wide", "narrow"),
        P("wide", "narrow"),
        P("wide", "narrow"),
        P("wide", "narrow"),
        P(),
        P(),
        P(),
        P(),
        P("narrow", "wide"),
        P(),
        P("wide", "narrow"),
        P("wide", "narrow"),
        P("narrow", "wide"),
    )
    return jax.shard_map(shards, mesh=mesh, in_specs=in_specs, out_specs=out_specs, check_vma=False)
```

profile of v0, /device:TPU:0, one launch (start us, length us, event | category | flops | bytes accessed | tf_op | source)
XLA Modules:
  0.0 1668.0 jit_solution(12426108417603169159)
XLA Ops:
  14.0 42.4 %all-gather.8.cloned.1.call-done = bf16[2560,1024]{1,0:T(8,128)(2,1)} async-done(((bf16[640,1024]{1,0:T(8,128)(2,1)}), bf16[2560,1024]{1,0:T(8,128)(2,1)}) %all-gather.8.cloned.1.call-update) | async-done | bytes 5242896 | tf_op jit(solution)/shard_map/all_gather | solution.py:177
  56.4 3.9 fusion.66
  60.4 3.6 fusion.63
  65.5 20.7 %all-gather.3 = bf16[8,1,128]{2,1,0:T(2,128)(2,1)S(1)} all-gather(bf16[1,1,128]{2,1,0:T(2,128)(2,1)S(1)} %convert_bitcast_fusion), channel_id=2, replica_groups=mesh['wide'=8,'narrow'=4] {'wide'}, dimensions={0}, use_global_device_ids=true | all-gather | bytes 2304 | tf_op jit(solution)/shard_map/all_gather | solution.py:18
  94.5 4.7 fusion.46
  102.2 95.5 %while.76 = (s32[]{:T(128)}, f32[128,256]{1,0:T(8,128)S(1)}, f32[40,128,256]{2,1,0:T(8,128)}, f32[40,128]{1,0:T(8,128)}, f32[40,128,256]{2,1,0:T(8,128)}, /*index=5*/s32[]{:T(128)}, s32[]{:T(128)}) while((s32[]{:T(128)}, f32[128,256]{1,0:T(8,128)S(1)}, f32[40,128,256]{2,1,0:T(8,128)}, f32[40,128]{1,0:T(8,128)}, ...), condition=%wide.region_3.4_spmd.clone, body=%wide.region_2.3_spmd.clone.sunk | while | flops 131075 | bytes 657004 | solution.py:117
  197.8 4.9 convolution_select_fusion
  202.7 7.1 fusion.67
  209.8 33.5 %all-gather.1 = bf16[1024,256]{1,0:T(8,128)(2,1)} all-gather(bf16[128,256]{1,0:T(8,128)(2,1)S(1)} %convert_element_type.188), channel_id=3, replica_groups=mesh['wide'=8,'narrow'=4] {'wide'}, dimensions={0}, use_global_device_ids=true | all-gather | bytes 589824 | tf_op jit(solution)/shard_map/all_gather | solution.py:18
  243.3 8.4 while.77
  251.7 4.0 convolution_add_fusion.2
  258.2 3.2 multiply_convert_fusion.4
  263.8 3.2 convert_element_type.191
  267.8 98.2 %all-reduce.5.cloned.1.call-done = bf16[2560,1024]{1,0:T(8,128)(2,1)} async-done(((bf16[2560,1024]{1,0:T(8,128)(2,1)}), bf16[2560,1024]{1,0:T(8,128)(2,1)}) %all-reduce.5.cloned.1.call-update) | async-done | bytes 5242896 | tf_op jit(solution)/shard_map/psum | solution.py:201
  366.1 3.7 multiply_reduce_fusion
  370.1 8.1 fusion.59
  378.2 6.3 fusion.60
  384.5 23.8 %all-gather.10.cloned.1.call-done = bf16[2560,1024]{1,0:T(8,128)(2,1)} async-done(((bf16[640,1024]{1,0:T(8,128)(2,1)}), bf16[2560,1024]{1,0:T(8,128)(2,1)}) %all-gather.10.cloned.1.call-update) | async-done | bytes 5242896 | tf_op jit(solution)/shard_map/all_gather | solution.py:220
  408.3 13.1 multiply_convert_fusion.1
  421.4 4.3 fusion.69
  425.7 8.8 add_convert_fusion.1
  434.7 9.2 convert_element_type.192
  443.9 42.2 %reduce-scatter.14.cloned.1.call-done = bf16[640,1024]{1,0:T(8,128)(2,1)} async-done(((bf16[2560,1024]{1,0:T(8,128)(2,1)}), bf16[640,1024]{1,0:T(8,128)(2,1)}) %reduce-scatter.14.cloned.1.call-update) | async-done | bytes 1310736 | tf_op jit(solution)/shard_map/reduce_scatter | solution.py:230
  486.1 3.7 fusion.20
  489.8 3.6 fusion.56
  496.4 143.0 %while.73 = (s32[]{:T(128)}, f32[128,256]{1,0:T(8,128)S(1)}, f32[40,128,256]{2,1,0:T(8,128)}, f32[40,128,1]{1,2,0:T(1,128)}, f32[40,128]{1,0:T(8,128)}, /*index=5*/f32[40,128,256]{2,1,0:T(8,128)}, s32[]{:T(128)}) while((s32[]{:T(128)}, f32[128,256]{1,0:T(8,128)S(1)}, f32[40,128,256]{2,1,0:T(8,128)}, f32[40,128,1]{1,2,0:T(1,128)}, ...), condition=%wide.region_16.17_spmd, body=%wide.region_15.16_spmd.sunk | while | flops 65538 | bytes 658021 | solution.py:117
  639.5 7.2 multiply_reduce_fusion.1
  646.7 3.1 add_add_fusion
  654.7 6.3 fusion.72
  661.0 31.4 %all-gather.2 = bf16[1024,256]{1,0:T(8,128)(2,1)S(1)} all-gather(bf16[128,256]{1,0:T(8,128)(2,1)S(1)} %fusion.43), channel_id=4, replica_groups=mesh['wide'=8,'narrow'=4] {'wide'}, dimensions={0}, use_global_device_ids=true | all-gather | bytes 589824 | tf_op jit(solution)/shard_map/all_gather | solution.py:43
  692.4 5.9 while.74
  698.2 9.9 fusion.70
  708.7 3.0 broadcast.122
  711.8 148.0 %while.75 = (s32[]{:T(128)}, f32[128,256]{1,0:T(8,128)S(1)}, f32[40,128]{1,0:T(8,128)}, f32[40,128,256]{2,1,0:T(8,128)}, f32[40,128,256]{2,1,0:T(8,128)}, /*inde...) while((s32[]{:T(128)}, f32[128,256]{1,0:T(8,128)S(1)}, ...), condition=%wide.region_21.22_spmd, body=%wide.region_19.21_spmd.sunk | while | flops 130947 | bytes 789633 | solution.py:117
  859.8 7.3 fusion.47
  867.1 4.9 fusion.45
  872.0 5.0 fusion.80
  877.3 5.5 add_convert_fusion.2
  885.5 3.3 fusion.35
  893.8 5.9 fusion.74
  899.8 5.4 fusion.75
  905.2 5.4 fusion.71
  910.6 5.5 fusion.73
  916.1 16.8 %add_convert_fusion = bf16[2560,1024]{1,0:T(8,128)(2,1)} fusion(f32[2560,1024]{1,0:T(8,128)} %fusion.75, f32[2560,1024]{1,0:T(8,128)} %fusion.74, f32[2560,1024]{1,0:T(8,128)} %fusion.71, f32[2560,1024]{1,0:T(8,128)} %fusion.73, bf16[2560,16]{0,1:T(8,128)(2,1)S(1)} %convolution_convert_fusion.4, bf16[1024,16]{0,1:T(8,128)(2,1)S(1)} %copy-done.51), kind=kOutput, calls=%fused_computation.20 | convolution fusion | flops 96993280 | bytes 47300608 | tf_op jit(solution)/shard_map/dot_general | solution.py:74
  933.0 8.1 convolution_convert_fusion
  941.2 9.6 convolution_bitcast_fusion
  951.5 9.2 fusion.58
  960.7 9.2 fusion.57
  970.0 4.0 fusion.81
  974.1 4.9 fusion.77
  979.1 5.0 fusion.76
  984.2 5.0 fusion.79
  989.5 5.5 fusion.78
  1001.5 38.2 %all-reduce.1 = (f32[1024]{0:T(1024)}, f32[16,512]{1,0:T(8,128)}, f32[512]{0:T(512)}, f32[256]{0:T(256)}, f32[1024]{0:T(1024)}) all-reduce(f32[1024]{0:T(1024)S(1)} %get-tuple-element.493, f32[16,512]{1,0:T(8,128)S(1)} %convolution_dynamic-update-slice_fusion, ...), channel_id=1, replica_groups=mesh['wide'=8,'narrow'=4] {'wide','narrow'}, use_global_device_ids=true, to_apply=%region_27.28 | all-reduce | flops 11008 | bytes 88064 | tf_op jit(solution)/shard_map/psum | solution.py:294
  1039.8 5.4 reduce-scatter.12.cloned.1.call-done
  1045.1 5.3 fusion.16
  1050.5 71.0 %reduce-scatter.32.cloned.1.call-done = f32[128,704]{0,1:T(8,128)} async-done(((f32[1024,704]{0,1:T(8,128)}), f32[128,704]{0,1:T(8,128)}) %reduce-scatter.32.cloned.1.call-update) | async-done | bytes 360464 | tf_op jit(solution)/shard_map/reduce_scatter | solution.py:286
  1121.5 75.4 %reduce-scatter.30.cloned.1.call-done = f32[128,704]{0,1:T(8,128)} async-done(((f32[1024,704]{0,1:T(8,128)}), f32[128,704]{0,1:T(8,128)}) %reduce-scatter.30.cloned.1.call-update) | async-done | bytes 360464 | tf_op jit(solution)/shard_map/reduce_scatter | solution.py:285
  1196.9 75.6 %reduce-scatter.28.cloned.1.call-done = f32[128,704]{0,1:T(8,128)} async-done(((f32[1024,704]{0,1:T(8,128)}), f32[128,704]{0,1:T(8,128)}) %reduce-scatter.28.cloned.1.call-update) | async-done | bytes 360464 | tf_op jit(solution)/shard_map/reduce_scatter | solution.py:284
  1272.5 122.7 %all-reduce.7.cloned.1.call-done = f32[1024,16]{0,1:T(8,128)} async-done(((f32[1024,16]{0,1:T(8,128)}), f32[1024,16]{0,1:T(8,128)}) %all-reduce.7.cloned.1.call-update) | async-done | bytes 65552 | tf_op jit(solution)/shard_map/psum | solution.py:294
  1395.2 66.7 %reduce-scatter.20.cloned.1.call-done = f32[128,128]{1,0:T(8,128)} async-done(((f32[1024,128]{1,0:T(8,128)}), f32[128,128]{1,0:T(8,128)}) %reduce-scatter.20.cloned.1.call-update) | async-done | bytes 65552 | tf_op jit(solution)/shard_map/reduce_scatter | solution.py:280
  1461.9 65.1 %reduce-scatter.18.cloned.1.call-done = f32[128,128]{1,0:T(8,128)} async-done(((f32[1024,128]{1,0:T(8,128)}), f32[128,128]{1,0:T(8,128)}) %reduce-scatter.18.cloned.1.call-update) | async-done | bytes 65552 | tf_op jit(solution)/shard_map/reduce_scatter | solution.py:279
  1527.0 66.2 %reduce-scatter.24.cloned.1.call-done = f32[128,256]{1,0:T(8,128)} async-done(((f32[1024,256]{1,0:T(8,128)}), f32[128,256]{1,0:T(8,128)}) %reduce-scatter.24.cloned.1.call-update) | async-done | bytes 131088 | tf_op jit(solution)/shard_map/reduce_scatter | solution.py:282
  1593.2 66.6 %reduce-scatter.22.cloned.1.call-done = f32[128,256]{1,0:T(8,128)} async-done(((f32[1024,256]{1,0:T(8,128)}), f32[128,256]{1,0:T(8,128)}) %reduce-scatter.22.cloned.1.call-update) | async-done | bytes 131088 | tf_op jit(solution)/shard_map/reduce_scatter | solution.py:281
  (720 shorter events, 447.7 us)
Async XLA Ops:
  7.2 401.1 %copy-start = (bf16[704,1024]{1,0:T(8,128)(2,1)S(1)}, bf16[704,1024]{1,0:T(8,128)(2,1)}, u32[]{:S(2)}) copy-start(bf16[704,1024]{1,0:T(8,128)(2,1)} %param.43) | copy-start | bytes 4325380
  7.2 49.2 %all-gather.8.cloned.1.call-start = ((), (), s32[]{:S(2)}) async-start(), calls=%async_computation.11 | async-start | bytes 6553600 | tf_op jit(solution)/shard_map/all_gather | solution.py:177
  8.0 5.8 copy-start.71
  8.0 5.8 copy-start.70
  8.0 48.4 %copy-start.50 = (bf16[1024,16]{0,1:T(8,128)(2,1)S(1)}, bf16[1024,16]{0,1:T(8,128)(2,1)}, u32[]{:S(2)}) copy-start(bf16[1024,16]{0,1:T(8,128)(2,1)} %param.35) | copy-start | bytes 98308
  13.1 353.0 %all-reduce.5.cloned.1.call-start = ((), (), s32[]{:S(2)}) async-start(), calls=%async_computation.12 | async-start | bytes 10485760 | tf_op jit(solution)/shard_map/psum | solution.py:201
  13.8 244.3 %copy-start.65 = (f32[256]{0:T(256)}, f32[256]{0:T(256)S(1)}, u32[]{:S(2)}) copy-start(f32[256]{0:T(256)S(1)} %convert_element_type.189) | copy-start | bytes 3076
  60.4 26.3 %slice-start = ((s8[5242880]{0:T(1024)(128)(4,1)}), s8[4194304]{0:T(1024)(128)(4,1)S(1)}, s32[]{:S(2)}) async-start(s8[5242880]{0:T(1024)(128)(4,1)} %bitcast.185), calls=%async_computation.27 | async-start | bytes 8388608
  64.0 22.7 %slice-start.1 = ((s8[5242880]{0:T(1024)(128)(4,1)}), s8[1048576]{0:T(1024)(128)(4,1)S(1)}, s32[]{:S(2)}) async-start(s8[5242880]{0:T(1024)(128)(4,1)} %bitcast.185), calls=%async_computation.28 | async-start | bytes 2097152
  64.8 133.0 %copy-start.1 = (f32[40,64,128]{2,0,1:T(8,128)}, f32[40,64,128]{2,0,1:T(8,128)S(1)}, u32[]{:S(2)}) copy-start(f32[40,64,128]{2,0,1:T(8,128)S(1)} %fusion.41) | copy-start | bytes 3932164
  86.2 8.3 copy-start.46
  94.5 4.7 copy-start.10
  197.8 4.9 copy-start.6
  202.7 40.6 %copy-start.31 = (f32[128,256]{1,0:T(8,128)S(1)}, f32[128,256]{1,0:T(8,128)}, u32[]{:S(2)}) copy-start(f32[128,256]{1,0:T(8,128)} %custom-call.1) | copy-start | bytes 393220
  243.3 14.9 slice-start.2
  251.7 6.5 slice-start.3
  267.0 141.2 %all-gather.10.cloned.1.call-start = ((), (), s32[]{:S(2)}) async-start(), calls=%async_computation.14 | async-start | bytes 6553600 | tf_op jit(solution)/shard_map/all_gather | solution.py:220
  267.8 218.3 %reduce-scatter.14.cloned.1.call-start = ((), (), s32[]{:S(2)}) async-start(), calls=%async_computation.15 | async-start | bytes 6553600 | tf_op jit(solution)/shard_map/reduce_scatter | solution.py:230
  370.1 64.5 %copy-start.59 = (f32[2560]{0:T(1024)}, f32[2560]{0:T(1024)S(1)}, u32[]{:S(2)}) copy-start(f32[2560]{0:T(1024)S(1)} %add_rsqrt_fusion) | copy-start | bytes 30724
  370.1 8.1 copy-start.67
  408.3 13.1 copy-start.68
  421.3 4.3 copy-start.72
  421.3 4.3 copy-start.69
  434.5 205.0 %all-gather.12.cloned.1.call-start = ((), (), s32[]{:S(2)}) async-start(), calls=%async_computation.16 | async-start | bytes 6553600 | tf_op jit(solution)/shard_map/all_gather | solution.py:239
  493.5 504.0 %reduce-scatter.26.cloned.1.call-start = ((), (), s32[]{:S(2)}) async-start(), calls=%async_computation.23 | async-start | bytes 1179648 | tf_op jit(solution)/shard_map/reduce_scatter | solution.py:283
  496.4 143.1 %copy-start.41 = (bf16[256,1024]{1,0:T(8,128)(2,1)S(1)}, bf16[256,1024]{1,0:T(8,128)(2,1)}, u32[]{:S(2)}) copy-start(bf16[256,1024]{1,0:T(8,128)(2,1)} %param.39) | copy-start | bytes 1572868
  496.4 143.1 %copy-start.66 = (f32[256]{0:T(256)S(1)}, f32[256]{0:T(256)}, u32[]{:S(2)}) copy-start(f32[256]{0:T(256)} %copy-done.65) | copy-start | bytes 3076
  639.5 7.2 copy-start.21
  639.5 7.2 copy-start.32
  649.9 4.8 copy-start.3
  708.7 151.0 %copy-start.2 = (f32[40,64,128]{2,0,1:T(8,128)S(1)}, f32[40,64,128]{2,0,1:T(8,128)}, u32[]{:S(2)}) copy-start(f32[40,64,128]{2,0,1:T(8,128)} %copy-done.1) | copy-start | bytes 3932164
  859.8 7.3 slice-start.4
  859.8 7.3 slice-start.5
  859.8 7.3 copy-start.47
  867.1 4.9 copy-start.34
  877.0 122.2 %reduce-scatter.16.cloned.1.call-start = ((), (), s32[]{:S(2)}) async-start(), calls=%async_computation.17 | async-start | bytes 6553600 | tf_op jit(solution)/shard_map/reduce_scatter | solution.py:270
  877.3 5.6 copy-start.16
  877.3 5.6 copy-start.29
  882.9 10.9 copy-start.28
  888.7 16.4 copy-start.22
  888.8 21.9 %copy-start.24 = (bf16[40,64,128]{2,1,0:T(8,128)(2,1)}, bf16[40,64,128]{2,1,0:T(8,128)(2,1)S(1)}, u32[]{:S(2)}) copy-start(bf16[40,64,128]{2,1,0:T(8,128)(2,1)S(1)} %get-tuple-element.570) | copy-start | bytes 1966084
  893.8 6.0 copy-start.26
  893.8 5.9 copy-start.45
  899.8 5.4 copy-start.37
  905.2 5.4 copy-start.49
  910.6 5.5 copy-start.51
  933.0 112.2 %reduce-scatter.12.cloned.1.call-start = ((), (), s32[]{:S(2)}) async-start(), calls=%async_computation.13 | async-start | bytes 6553600 | tf_op jit(solution)/shard_map/reduce_scatter | solution.py:213
  941.1 180.4 %reduce-scatter.32.cloned.1.call-start = ((), (), s32[]{:S(2)}) async-start(), calls=%async_computation.26 | async-start | bytes 3244032 | tf_op jit(solution)/shard_map/reduce_scatter | solution.py:286
  950.8 246.1 %reduce-scatter.30.cloned.1.call-start = ((), (), s32[]{:S(2)}) async-start(), calls=%async_computation.25 | async-start | bytes 3244032 | tf_op jit(solution)/shard_map/reduce_scatter | solution.py:285
  960.7 311.8 %reduce-scatter.28.cloned.1.call-start = ((), (), s32[]{:S(2)}) async-start(), calls=%async_computation.24 | async-start | bytes 3244032 | tf_op jit(solution)/shard_map/reduce_scatter | solution.py:284
  970.0 425.2 %all-reduce.7.cloned.1.call-start = ((), (), s32[]{:S(2)}) async-start(), calls=%async_computation.22 | async-start | bytes 131072 | tf_op jit(solution)/shard_map/psum | solution.py:294
  974.0 5.1 copy-start.23
  974.0 487.8 %reduce-scatter.20.cloned.1.call-start = ((), (), s32[]{:S(2)}) async-start(), calls=%async_computation.19 | async-start | bytes 589824 | tf_op jit(solution)/shard_map/reduce_scatter | solution.py:280
  979.1 5.1 copy-start.27
  979.1 547.9 %reduce-scatter.18.cloned.1.call-start = ((), (), s32[]{:S(2)}) async-start(), calls=%async_computation.18 | async-start | bytes 589824 | tf_op jit(solution)/shard_map/reduce_scatter | solution.py:279
  984.1 609.1 %reduce-scatter.24.cloned.1.call-start = ((), (), s32[]{:S(2)}) async-start(), calls=%async_computation.21 | async-start | bytes 1179648 | tf_op jit(solution)/shard_map/reduce_scatter | solution.py:282
  989.2 6.1 copy-start.39
  989.2 670.5 %reduce-scatter.22.cloned.1.call-start = ((), (), s32[]{:S(2)}) async-start(), calls=%async_computation.20 | async-start | bytes 1179648 | tf_op jit(solution)/shard_map/reduce_scatter | solution.py:281
  994.9 4.3 copy-start.5
  994.9 4.3 copy-start.54
  994.9 4.3 copy-start.56
  994.9 6.6 copy-start.61
  994.9 6.6 copy-start.64
  995.0 50.2 %copy-start.58 = (f32[640]{0:T(1024)S(1)}, f32[640]{0:T(1024)}, u32[]{:S(2)}) copy-start(f32[640]{0:T(1024)} %copy-done.57) | copy-start | bytes 7684
  (31 other events, 75.0 us)
Sparse Core Ops, SparseCore 0:
  13.2 43.1 all-gather.7
  267.1 98.8 all-reduce.4
  367.6 40.5 all-gather.9
  434.6 51.3 reduce-scatter.13
  493.6 40.4 all-gather.11
  877.1 60.0 reduce-scatter.25
  939.8 50.3 reduce-scatter.15
  992.9 52.1 reduce-scatter.11
  1049.3 72.1 reduce-scatter.31
  1125.5 71.3 reduce-scatter.29
  1201.0 71.3 reduce-scatter.27
  1278.5 116.6 all-reduce.6
  1399.1 62.7 reduce-scatter.19
  1466.0 60.9 reduce-scatter.17
  1530.8 62.3 reduce-scatter.23
  1597.4 62.3 reduce-scatter.21
where the time goes:
time: 1690 us; the launch traced here: 1670 us
  waiting for transfers between devices  822 us (49%)
  local copies, waits for them, and re-layouts  253 us (15%)
  matrix products  241 us (14%)
  other arithmetic  207 us (12%)
  blocking collectives  124 us (7%)
    dynamic_update_slice x160, local copies, waits for them, and re-layouts, segment_mix(): lax.scan(advance, start_state, (block_rates, block_states))  153 us
    psum x1, waiting for transfers between devices, shards(): lax.psum((norm_gain_part, mlp_gain_part, group_part, grad_rank_down, rank...  123 us
    psum x1, waiting for transfers between devices, shards(): lax.psum(full_term.astype(jnp.bfloat16), 'narrow').astype(jnp.float32)  98.2 us
    mul x120, local copies, waits for them, and re-layouts, advance(): return (decay_rate[:, None] * carried + increment, carried)  82 us
    add x80, other arithmetic, advance(): return (decay_rate[:, None] * carried + increment, carried)  79.5 us
    reduce_scatter x1, waiting for transfers between devices, shards(): lax.psum_scatter(grad_mlp_gate, 'wide', scatter_dimension=0, tiled=True)  75.6 us
    reduce_scatter x1, waiting for transfers between devices, shards(): lax.psum_scatter(grad_mlp_up, 'wide', scatter_dimension=0, tiled=True)  75.4 us
    dot_general x9, matrix products, matmul_nt(): lax.dot_general(left_mat, right_mat, (((1,), (1,)), ((), ())), preferred_...  72.4 us
  transfers between devices with their start and end apart: 16, of which 13 were waited for; matrix products, arithmetic and copies ran while one was open for 18% of the time, Pallas kernels for 0%

commit v1 on v0

v1 whole, which is shorter than its diff:
```python
import functools

import jax
import jax.numpy as jnp
from jax import lax
from jax.experimental import pallas as pl
from jax.experimental.pallas import tpu as pltpu
from jax.sharding import PartitionSpec as P

NORM_EPS = 1e-06
GROUP_EPS = 1e-05
GATE_NORM = 16.0
HIGHEST_PREC = lax.Precision.HIGHEST
CHUNK = 128
HALF = CHUNK // 2
BLOCK = 256
F32 = jnp.float32
BF16 = jnp.bfloat16


def dot(a, b):
    return lax.dot_general(a, b, (((1,), (0,)), ((), ())), preferred_element_type=F32)


def dot_nt(a, b):
    return lax.dot_general(a, b, (((1,), (1,)), ((), ())), preferred_element_type=F32)


def dot_tn(a, b):
    return lax.dot_general(a, b, (((0,), (0,)), ((), ())), preferred_element_type=F32)


def exact(a, b, dims):
    return lax.dot_general(
        a, b, (dims, ((), ())), precision=HIGHEST_PREC, preferred_element_type=F32
    )


def sds(shape, dtype):
    return jax.ShapeDtypeStruct(shape, dtype)


def params(mib=48):
    return pltpu.CompilerParams(vmem_limit_bytes=mib << 20)


def cost(flops, nbytes, trans=0):
    return pl.CostEstimate(flops=int(flops), bytes_accessed=int(nbytes), transcendentals=int(trans))


def whole(shape):
    return pl.BlockSpec(shape, lambda i: (0,) * len(shape), pipeline_mode=pl.Buffered(1))


def rows_spec(rows, cols):
    return pl.BlockSpec((rows, cols), lambda i: (i, 0))


def triangle(lower):
    r = lax.broadcasted_iota(jnp.int32, (CHUNK, CHUNK), 0)
    c = lax.broadcasted_iota(jnp.int32, (CHUNK, CHUNK), 1)
    return r >= c if lower else r <= c


def forward_head_kernel(
    x_ref, w_ref, rd_ref, ru_ref, bias_ref,
    q_ref, k_ref, v_ref, s_ref, cum_ref, dpre_ref, rank_ref, base_ref, reach_ref, sin_ref, off_ref,
    state_ref, mult_ref,
    st, off,
):
    i = pl.program_id(0)
    dk = q_ref.shape[1]
    dv = v_ref.shape[1]

    @pl.when(i == 0)
    def _():
        st[...] = jnp.zeros_like(st)
        off[...] = jnp.zeros_like(off)

    x = x_ref[...]
    proj = dot(x, w_ref[...])
    rank = dot(x, rd_ref[...])
    dpre = exact(rank, ru_ref[...], ((1,), (0,))) + bias_ref[...]
    dlog = jax.nn.log_sigmoid(dpre) * (1.0 / GATE_NORM)
    q_low = proj[:, :dk].astype(BF16)
    k_low = proj[:, dk : 2 * dk].astype(BF16)
    v_low = proj[:, 2 * dk : 2 * dk + dv].astype(BF16)
    q_ref[...] = q_low
    k_ref[...] = k_low
    v_ref[...] = v_low
    s_ref[...] = proj[:, 2 * dk + dv :]
    rank_ref[...] = rank
    dpre_ref[...] = dpre
    mask = triangle(True)
    ones = mask.astype(F32)
    scale = dk**-0.5
    for j in range(BLOCK // CHUNK):
        rows = slice(j * CHUNK, (j + 1) * CHUNK)
        cum = exact(ones, dlog[rows], ((1,), (0,)))
        mid = cum[HALF - 1 : HALF]
        end = cum[CHUNK - 1 :]
        qf = q_low[rows].astype(F32) * scale
        kf = k_low[rows].astype(F32)
        v = v_low[rows]
        qd = (qf * jnp.exp(cum - mid)).astype(BF16)
        kd = (kf * jnp.exp(mid - cum)).astype(BF16)
        qi = (qf * jnp.exp(cum)).astype(BF16)
        ke = (kf * jnp.exp(end - cum)).astype(BF16)
        scores = jnp.where(mask, dot_nt(qd, kd), 0.0).astype(BF16)
        state = st[...]
        state_low = state.astype(BF16)
        offset = off[...]
        base_ref[rows, :] = dot(scores, v) + dot_nt(qi, state_low)
        reach_ref[rows, :] = (qf * jnp.exp(cum + offset)).astype(BF16)
        cum_ref[rows, :] = cum
        sin_ref[j] = state_low
        off_ref[j] = offset
        st[...] = state * jnp.exp(end) + dot_tn(v, ke)
        off[...] = offset + end
    state_ref[...] = st[...]
    mult_ref[...] = jnp.exp(off[...])


def forward_head(x, w, rank_down, rank_cols, bias_cols, dk, dv):
    n, d = x.shape
    rank = rank_down.shape[1]
    per = BLOCK // CHUNK
    return pl.pallas_call(
        forward_head_kernel,
        name="forward_head",
        grid=(n // BLOCK,),
        in_specs=[
            rows_spec(BLOCK, d), whole(w.shape), whole(rank_down.shape), whole(rank_cols.shape), whole(bias_cols.shape),
        ],
        out_specs=[
            rows_spec(BLOCK, dk), rows_spec(BLOCK, dk), rows_spec(BLOCK, dv), rows_spec(BLOCK, dv),
            rows_spec(BLOCK, dk), rows_spec(BLOCK, dk), rows_spec(BLOCK, rank), rows_spec(BLOCK, dv), rows_spec(BLOCK, dk),
            pl.BlockSpec((per, dv, dk), lambda i: (i, 0, 0)), pl.BlockSpec((per, 1, dk), lambda i: (i, 0, 0)),
            whole((dv, dk)), whole((1, dk)),
        ],
        out_shape=[
            sds((n, dk), BF16), sds((n, dk), BF16), sds((n, dv), BF16), sds((n, dv), F32),
            sds((n, dk), F32), sds((n, dk), F32), sds((n, rank), F32), sds((n, dv), F32), sds((n, dk), BF16),
            sds((n // CHUNK, dv, dk), BF16), sds((n // CHUNK, 1, dk), F32),
            sds((dv, dk), F32), sds((1, dk), F32),
        ],
        scratch_shapes=[pltpu.VMEM((dv, dk), F32), pltpu.VMEM((1, dk), F32)],
        compiler_params=params(),
        cost_estimate=cost(2 * n * d * (2 * dk + 2 * dv) * 1.5, n * d * 2 + n * 4000, n * dk * 6),
    )(x, w, rank_down, rank_cols, bias_cols)


def gate_out_kernel(b0, b1, r0, r1, s0, s1, e0, e1, gain_ref, w0, w1, m0, m1, g0, g1, out_ref):
    total = None
    gain = gain_ref[...]
    for b, r, s, e, w, m, g in ((b0, r0, s0, e0, w0, m0, g0), (b1, r1, s1, e1, w1, m1, g1)):
        mixed = b[...] + dot_nt(r[...], e[...])
        inv = lax.rsqrt(jnp.mean(mixed * mixed, axis=-1, keepdims=True) + GROUP_EPS)
        sw = s[...]
        gated = (mixed * inv * gain * (sw * jax.nn.sigmoid(sw))).astype(BF16)
        m[...] = mixed
        g[...] = gated
        part = dot(gated, w[...])
        total = part if total is None else total + part
    out_ref[...] = total.astype(BF16)


def gate_out(bases, reaches, swishes, enters, gain, weights):
    n, dv = bases[0].shape
    dk = reaches[0].shape[1]
    d = weights[0].shape[1]
    row = rows_spec(BLOCK, dv)
    return pl.pallas_call(
        gate_out_kernel,
        name="gate_out",
        grid=(n // BLOCK,),
        in_specs=[row, row, rows_spec(BLOCK, dk), rows_spec(BLOCK, dk), row, row]
        + [whole((dv, dk))] * 2 + [whole((1, dv))] + [whole((dv, d))] * 2,
        out_specs=[row, row, row, row, rows_spec(BLOCK, d)],
        out_shape=[sds((n, dv), F32)] * 2 + [sds((n, dv), BF16)] * 2 + [sds((n, d), BF16)],
        compiler_params=params(),
        cost_estimate=cost(2 * n * dv * (d + dk) * 2, n * (dv * 28 + d * 2), n * dv * 2),
    )(*bases, *reaches, *swishes, *enters, gain, *weights)


def mlp_kernel(x_ref, c_ref, wg_ref, wu_ref, wd_ref, h_ref, gg_ref, gu_ref, dn_ref, gn_ref):
    x = x_ref[...]
    gate = dot(x, wg_ref[...])
    up = dot(x, wu_ref[...])
    gh = dot_nt(c_ref[...], wd_ref[...])
    sig = jax.nn.sigmoid(gate)
    act = gate * sig
    hidden = (act * up).astype(BF16)
    g_up = (gh * act).astype(BF16)
    g_gate = (gh * up * sig * (1.0 + gate * (1.0 - sig))).astype(BF16)
    h_ref[...] = hidden
    gg_ref[...] = g_gate
    gu_ref[...] = g_up
    gn_ref[...] = (dot_nt(g_gate, wg_ref[...]) + dot_nt(g_up, wu_ref[...])).astype(BF16)
    dn_ref[...] = dot(hidden, wd_ref[...]).astype(BF16)


def mlp(x, cot, wg, wu, wd):
    n, d = x.shape
    ff = wg.shape[1]
    blk = 320 if n % 320 == 0 else n
    return pl.pallas_call(
        mlp_kernel,
        name="mlp",
        grid=(n // blk,),
        in_specs=[rows_spec(blk, d), rows_spec(blk, d), whole((d, ff)), whole((d, ff)), whole((ff, d))],
        out_specs=[rows_spec(blk, ff)] * 3 + [rows_spec(blk, d)] * 2,
        out_shape=[sds((n, ff), BF16)] * 3 + [sds((n, d), BF16)] * 2,
        compiler_params=params(),
        cost_estimate=cost(12 * n * d * ff, n * d * 8 + n * ff * 6 + d * ff * 6, n * ff),
    )(x, cot, wg, wu, wd)


def mlp_grads_kernel(pieces, *refs):
    xs, cs, hs, ggs, gus = [refs[i * pieces : (i + 1) * pieces] for i in range(5)]
    out_ref = refs[5 * pieces]
    ff = hs[0].shape[1]
    for at, lefts, rights in ((0, xs, ggs), (ff, xs, gus), (2 * ff, cs, hs)):
        acc = dot_tn(lefts[0][...], rights[0][...])
        for left, right in zip(lefts[1:], rights[1:]):
            acc = acc + dot_tn(left[...], right[...])
        out_ref[:, at : at + ff] = acc.astype(BF16)


def mlp_grads(xs, cs, hs, ggs, gus):
    pieces = len(xs)
    n, d = xs[0].shape
    ff = hs[0].shape[1]
    blk = 256
    cols = pl.BlockSpec((n, blk), lambda i: (0, i))
    return pl.pallas_call(
        functools.partial(mlp_grads_kernel, pieces),
        name="mlp_grads",
        grid=(d // blk,),
        in_specs=[cols] * (2 * pieces) + [whole((n, ff))] * (3 * pieces),
        out_specs=rows_spec(blk, 3 * ff),
        out_shape=sds((d, 3 * ff), BF16),
        compiler_params=params(),
        cost_estimate=cost(6 * pieces * n * d * ff, pieces * n * (d * 4 + ff * 6) + d * ff * 6),
    )(*xs, *cs, *hs, *ggs, *gus)


def gate_back_kernel(
    gm_ref, m0, m1, s0, s1, r0, r1, gain_ref, w0, w1, gx0, gx1, gs0, gs1, lb0, lb1, gp_ref
):
    i = pl.program_id(0)

    @pl.when(i == 0)
    def _():
        lb0[...] = jnp.zeros_like(lb0)
        lb1[...] = jnp.zeros_like(lb1)
        gp_ref[...] = jnp.zeros_like(gp_ref)

    gm = gm_ref[...]
    gain = gain_ref[...]
    for m, s, r, w, gx, gs, lb in ((m0, s0, r0, w0, gx0, gs0, lb0), (m1, s1, r1, w1, gx1, gs1, lb1)):
        grad = dot_nt(gm, w[...])
        mixed = m[...]
        inv = lax.rsqrt(jnp.mean(mixed * mixed, axis=-1, keepdims=True) + GROUP_EPS)
        unit = mixed * inv
        sw = s[...]
        sig = jax.nn.sigmoid(sw)
        gs[...] = (grad * unit * gain * (sig * (1.0 + sw * (1.0 - sig)))).astype(BF16)
        dn = grad * (sw * sig)
        gp_ref[...] += jnp.sum(dn * unit, axis=0, keepdims=True)
        weighted = dn * gain
        gmix = (inv * (weighted - unit * jnp.mean(weighted * unit, axis=-1, keepdims=True))).astype(BF16)
        gx[...] = gmix
        lb[...] += dot_tn(gmix, r[...])


def gate_back(gm, mixeds, swishes, reaches, gain, weights):
    n, d = gm.shape
    dv = mixeds[0].shape[1]
    dk = reaches[0].shape[1]
    row = rows_spec(BLOCK, dv)
    return pl.pallas_call(
        gate_back_kernel,
        name="gate_back",
        grid=(n // BLOCK,),
        in_specs=[rows_spec(BLOCK, d), row, row, row, row, rows_spec(BLOCK, dk), rows_spec(BLOCK, dk)]
        + [whole((1, dv))] + [whole((dv, d))] * 2,
        out_specs=[row] * 4 + [whole((dv, dk))] * 2 + [whole((1, dv))],
        out_shape=[sds((n, dv), BF16)] * 4 + [sds((dv, dk), F32)] * 2 + [sds((1, dv), F32)],
        compiler_params=params(),
        cost_estimate=cost(2 * n * dv * (d + dk) * 2, n * (dv * 28 + d * 2), n * dv * 2),
    )(gm, *mixeds, *swishes, *reaches, gain, *weights)


def back_head_kernel(
    q_ref, k_ref, v_ref, cum_ref, dpre_ref, rank_ref, sin_ref, off_ref, gx_ref, gs_ref, enter_ref, later_ref, ru_ref,
    all_ref, grank_ref, rup_ref, bias_ref,
    ds,
):
    i = pl.program_id(0)
    dk = q_ref.shape[1]
    dv = v_ref.shape[1]

    @pl.when(i == 0)
    def _():
        ds[...] = later_ref[...]
        rup_ref[...] = jnp.zeros_like(rup_ref)
        bias_ref[...] = jnp.zeros_like(bias_ref)

    mask = triangle(True)
    ones = triangle(False).astype(F32)
    scale = dk**-0.5
    enter = enter_ref[...]
    for j in reversed(range(BLOCK // CHUNK)):
        rows = slice(j * CHUNK, (j + 1) * CHUNK)
        cum = cum_ref[rows, :]
        mid = cum[HALF - 1 : HALF]
        end = cum[CHUNK - 1 :]
        e_qd, e_kd, e_qi, e_ke = jnp.exp(cum - mid), jnp.exp(mid - cum), jnp.exp(cum), jnp.exp(end - cum)
        e_end = jnp.exp(end)
        qf = q_ref[rows, :].astype(F32) * scale
        kf = k_ref[rows, :].astype(F32)
        v = v_ref[rows, :]
        qd = (qf * e_qd).astype(BF16)
        kd = (kf * e_kd).astype(BF16)
        qi = (qf * e_qi).astype(BF16)
        ke = (kf * e_ke).astype(BF16)
        go = gx_ref[rows, :]
        state = sin_ref[j].astype(F32) + enter * jnp.exp(off_ref[j])
        state_low = state.astype(BF16)
        dstate = ds[...]
        dstate_low = dstate.astype(BF16)
        scores = jnp.where(mask, dot_nt(qd, kd), 0.0).astype(BF16)
        dscores = jnp.where(mask, dot_nt(go, v), 0.0).astype(BF16)
        d_v = dot_tn(scores, go) + dot_nt(ke, dstate_low)
        d_qd = dot(dscores, kd)
        d_qi = dot(go, state_low)
        d_kd = dot_tn(dscores, qd)
        d_ke = dot(v, dstate_low)
        d_q = scale * (d_qd * e_qd + d_qi * e_qi)
        d_k = d_kd * e_kd + d_ke * e_ke
        tail = ke.astype(F32) * d_ke
        d_cum = qd.astype(F32) * d_qd + qi.astype(F32) * d_qi - kd.astype(F32) * d_kd - tail
        d_end = jnp.sum(tail, axis=0, keepdims=True) + e_end * jnp.sum(dstate * state, axis=0, keepdims=True)
        grad_decay = exact(ones, d_cum, ((1,), (0,))) + d_end
        g_pre = grad_decay * jax.nn.sigmoid(-dpre_ref[rows, :]) * (1.0 / GATE_NORM)
        all_ref[rows, :dk] = d_q.astype(BF16)
        all_ref[rows, dk : 2 * dk] = d_k.astype(BF16)
        all_ref[rows, 2 * dk : 2 * dk + dv] = d_v.astype(BF16)
        all_ref[rows, 2 * dk + dv :] = gs_ref[rows, :]
        grank_ref[rows, :] = exact(g_pre, ru_ref[...], ((1,), (1,)))
        rup_ref[...] += exact(rank_ref[rows, :], g_pre, ((0,), (0,)))
        bias_ref[...] += jnp.sum(g_pre, axis=0, keepdims=True)
        ds[...] = dstate * e_end + dot_tn(go, qi)


def back_head(q, k, v, cum, dpre, rank, sin, off, gx, gs, enter, later, rank_cols):
    n, dk = q.shape
    dv = v.shape[1]
    rk = rank.shape[1]
    per = BLOCK // CHUNK
    last = n // BLOCK - 1

    def rev(rows, cols):
        return pl.BlockSpec((rows, cols), lambda i: (last - i, 0))

    return pl.pallas_call(
        back_head_kernel,
        name="back_head",
        grid=(n // BLOCK,),
        in_specs=[
            rev(BLOCK, dk), rev(BLOCK, dk), rev(BLOCK, dv), rev(BLOCK, dk), rev(BLOCK, dk), rev(BLOCK, rk),
            pl.BlockSpec((per, dv, dk), lambda i: (last - i, 0, 0)), pl.BlockSpec((per, 1, dk), lambda i: (last - i, 0, 0)),
            rev(BLOCK, dv), rev(BLOCK, dv), whole((dv, dk)), whole((dv, dk)), whole((rk, dk)),
        ],
        out_specs=[rev(BLOCK, 2 * dk + 2 * dv), rev(BLOCK, rk), whole((rk, dk)), whole((1, dk))],
        out_shape=[sds((n, 2 * dk + 2 * dv), BF16), sds((n, rk), F32), sds((rk, dk), F32), sds((1, dk), F32)],
        scratch_shapes=[pltpu.VMEM((dv, dk), F32)],
        compiler_params=params(),
        cost_estimate=cost(n * 128 * 128 * 40, n * 6000, n * dk * 6),
    )(q, k, v, cum, dpre, rank, sin, off, gx, gs, enter, later, rank_cols)


def hop(value, axis, bit):
    return lax.ppermute(value, axis, [(i, i ^ bit) for i in range(lax.axis_size(axis))])


def wide_bits():
    count, bits, bit = lax.axis_size("wide"), [], 1
    while bit < count:
        bits.append(bit)
        bit *= 2
    return bits


def scan_states(mult, state, backward):
    place = {"narrow": lax.axis_index("narrow"), "wide": lax.axis_index("wide")}
    heads, dv, dk = state.shape
    pre_m, pre_s = jnp.ones_like(mult), jnp.zeros_like(state)
    tot_m, tot_s = mult, state
    for axis, bit in [("narrow", 2)] + [("wide", b) for b in wide_bits()]:
        packed = jnp.concatenate(
            [tot_s, jnp.broadcast_to(tot_m, (heads, 16, dk))], axis=1
        ).astype(BF16)
        other = hop(packed, axis, bit).astype(F32)
        if axis == "narrow":
            other = other[::-1]
        oth_s, oth_m = other[:, :dv], other[:, dv : dv + 1]
        is_set = (place[axis] & bit) != 0
        mine_later = jnp.logical_not(is_set) if backward else is_set
        new_s = oth_s * pre_m + pre_s
        new_m = oth_m * pre_m
        sum_later = oth_s * tot_m + tot_s
        sum_first = tot_s * oth_m + oth_s
        pre_s = jnp.where(mine_later, new_s, pre_s)
        pre_m = jnp.where(mine_later, new_m, pre_m)
        tot_s = jnp.where(mine_later, sum_later, sum_first)
        tot_m = tot_m * oth_m
    return pre_s


def scatter_rows(value, bits):
    count = lax.axis_size("wide")
    place = lax.axis_index("wide")
    rows, cols = value.shape[0] // count, value.shape[1]
    order = sorted(bits, reverse=True)
    value = value.reshape((2,) * len(bits) + (rows, cols))
    left = list(order)
    for bit in bits:
        dim = left.index(bit)
        mine = jnp.where((place & bit) != 0, 1, 0)
        keep = lax.dynamic_index_in_dim(value, mine, dim, False)
        send = lax.dynamic_index_in_dim(value, 1 - mine, dim, False)
        got = hop(send.astype(BF16), "wide", bit)
        value = keep.astype(F32) + got.astype(F32)
        left.pop(dim)
        if left:
            value = value.astype(BF16)
    return value


def sum_everywhere(value):
    for axis, bit in [("narrow", 1), ("narrow", 2)] + [("wide", b) for b in wide_bits()]:
        value = value + hop(value, axis, bit)
    return value


def norm_back(grad, values, inv, gain):
    unit = values * inv
    weighted = grad * gain
    part = jnp.sum(grad * unit, axis=0, keepdims=True)
    return inv * (weighted - unit * jnp.mean(weighted * unit, axis=-1, keepdims=True)), part


def shards(
    tokens, cotangent, flags, norm_gain, query_weight, key_weight, value_weight, swish_weight, rank_down, rank_up,
    decay_bias, group_gain, output_weight, mlp_gain, mlp_gate, mlp_up, mlp_down,
):
    own_rows = tokens.shape[0]
    place = lax.axis_index("narrow")
    core = place & 1
    second = (place & 2) != 0
    wide_odd = (lax.axis_index("wide") & 1) != 0
    dk = query_weight.shape[1]
    dv = value_weight.shape[1]
    d = tokens.shape[1]

    def in_order(mine, other):
        return jnp.where(
            core == 0, jnp.concatenate([mine, other]), jnp.concatenate([other, mine])
        )

    def from_row_partner(value):
        half = value.shape[0] // 2
        piece = lax.dynamic_slice_in_dim(value, jnp.where(wide_odd, half, 0), half, 0)
        first = hop(piece, "narrow", 2)
        relayed = hop(first, "wide", 1)
        return jnp.where(
            wide_odd, jnp.concatenate([relayed, first]), jnp.concatenate([first, relayed])
        )

    def head_cols(index):
        ru = lax.dynamic_slice_in_dim(rank_up, index * dk, dk, 1).astype(F32)
        bias = lax.dynamic_slice_in_dim(decay_bias, index * dk, dk, 0).astype(F32)
        return ru, bias.reshape(1, dk)

    restart = 1.0 - flags[0].astype(F32)
    restart = jnp.where(second, 1.0, restart)
    norm_gain_f = norm_gain.astype(F32)
    mlp_gain_f = mlp_gain.astype(F32)
    gain_row = group_gain.astype(F32).reshape(1, dv)

    inputs = tokens.astype(F32)
    inv_one = lax.rsqrt(jnp.mean(inputs * inputs, axis=-1, keepdims=True) + NORM_EPS)
    normed = (inputs * inv_one * norm_gain_f).astype(BF16)
    normed_two = hop(normed, "narrow", 1)
    rows_all = in_order(normed, normed_two)

    w_own = jnp.concatenate([query_weight, key_weight, value_weight, swish_weight], axis=1)
    w_other = from_row_partner(w_own)
    out_other = from_row_partner(output_weight)
    cot_late, w_other, out_other = lax.optimization_barrier((cotangent, w_other, out_other))
    cot_y = hop(cot_late, "narrow", 2)
    cot_c = hop(cotangent, "narrow", 1)
    cot_d = hop(cot_y, "narrow", 1)

    ru_own, bias_own = head_cols(place)
    ru_oth, bias_oth = head_cols(place ^ 2)
    weights_out = (output_weight, out_other)
    one = forward_head(rows_all, w_own, rank_down, ru_own, bias_own, dk, dv)
    two = forward_head(rows_all, w_other, rank_down, ru_oth, bias_oth, dk, dv)
    (q, k, v, s, cum, dpre, rank_pre, base, reach, sin, off, state, mult) = zip(one, two)
    rank_pre = rank_pre[0]
    mults = restart * jnp.stack(mult)
    enter = restart * scan_states(mults, jnp.stack(state), False)
    enter_low = enter.astype(BF16)
    mixed0, mixed1, gated0, gated1, term = gate_out(
        base, reach, s, (enter_low[0], enter_low[1]), gain_row, weights_out
    )
    own_term = lax.dynamic_slice_in_dim(term, core * own_rows, own_rows, 0)
    send_term = lax.dynamic_slice_in_dim(term, (1 - core) * own_rows, own_rows, 0)
    middle = inputs + (own_term.astype(F32) + hop(send_term, "narrow", 1).astype(F32))
    inv_two = lax.rsqrt(jnp.mean(middle * middle, axis=-1, keepdims=True) + NORM_EPS)
    x_own = (middle * inv_two * mlp_gain_f).astype(BF16)

    x_y = hop(x_own, "narrow", 2)
    x_c = hop(x_own, "narrow", 1)
    x_d = hop(x_y, "narrow", 1)
    xs, cs = (x_own, x_c, x_y, x_d), (cotangent, cot_c, cot_y, cot_d)
    hs, ggs, gus, dns, gns = zip(*[mlp(x, c, mlp_gate, mlp_up, mlp_down) for x, c in zip(xs, cs)])

    def gather_sum(parts):
        own, by_core, by_y, by_both = parts
        across = by_y.astype(F32) + hop(by_both, "narrow", 1).astype(F32)
        near = own.astype(F32) + hop(by_core, "narrow", 1).astype(F32)
        return near + hop(across.astype(BF16), "narrow", 2).astype(F32)

    grad_two = gather_sum(gns)
    mlp_w_grads = mlp_grads(xs, cs, hs, ggs, gus)
    bits = wide_bits()
    mlp_w = scatter_rows(mlp_w_grads, bits)

    grad_norm, mlp_gain_part = norm_back(grad_two, middle, inv_two, mlp_gain_f)
    grad_middle = cotangent.astype(F32) + grad_norm
    middle_low = grad_middle.astype(BF16)
    gm_all = in_order(middle_low, hop(middle_low, "narrow", 1))
    gx0, gx1, gs0, gs1, lb0, lb1, group_part = gate_back(
        gm_all, (mixed0, mixed1), s, reach, gain_row, weights_out
    )
    later = scan_states(mults, restart * jnp.stack([lb0, lb1]), True)
    dns_y, _ = lax.optimization_barrier((dns, gm_all))
    result = (middle + gather_sum(dns_y)).astype(BF16)

    all0, gr0, rup0, gb0 = back_head(
        q[0], k[0], v[0], cum[0], dpre[0], rank_pre, sin[0], off[0], gx0, gs0, enter[0], later[0], ru_own
    )
    all1, gr1, rup1, gb1 = back_head(
        q[1], k[1], v[1], cum[1], dpre[1], rank_pre, sin[1], off[1], gx1, gs1, enter[1], later[1], ru_oth
    )
    grad_rank = (gr0 + gr1).astype(BF16)
    total = dot_nt(all0, w_own) + dot_nt(all1, w_other) + dot_nt(grad_rank, rank_down)
    total = total.astype(BF16)
    own_total = lax.dynamic_slice_in_dim(total, core * own_rows, own_rows, 0)
    send_total = lax.dynamic_slice_in_dim(total, (1 - core) * own_rows, own_rows, 0)
    grad_normed = own_total.astype(F32) + hop(send_total, "narrow", 1).astype(F32)
    grad_input, norm_gain_part = norm_back(grad_normed, inputs, inv_one, norm_gain_f)
    input_grad = grad_middle + grad_input

    def over_y(mine, other):
        return (mine + hop(other.astype(BF16), "narrow", 2).astype(F32)).astype(BF16)

    qkvs = over_y(dot_tn(rows_all, all0), dot_tn(rows_all, all1))
    outs = over_y(dot_tn(gm_all, gated0), dot_tn(gm_all, gated1))
    qkvs = scatter_rows(qkvs, bits)
    outs = scatter_rows(outs, bits)
    grad_rank_down = dot_tn(rows_all, grad_rank)

    def spread(mine, other, width):
        zero = jnp.zeros((mine.shape[0], width), F32)
        zero = lax.dynamic_update_slice_in_dim(zero, mine, place * dk, 1)
        return lax.dynamic_update_slice_in_dim(zero, other, (place ^ 2) * dk, 1)

    qk = rank_up.shape[1]
    rank = rank_up.shape[0]
    small = [
        norm_gain_part,
        mlp_gain_part,
        group_part,
        grad_rank_down.T,
        spread(rup0, rup1, qk),
        spread(gb0, gb1, qk),
    ]
    flat = jnp.concatenate([jnp.reshape(part, (-1, dk)) for part in small])
    flat = sum_everywhere(flat)
    parts, at = [], 0
    for part in small:
        size = part.size // dk
        parts.append(flat[at : at + size].reshape(part.shape))
        at += size
    ff = mlp_gate.shape[1]
    return (
        result,
        input_grad,
        parts[0].reshape(d),
        qkvs[:, :dk],
        qkvs[:, dk : 2 * dk],
        qkvs[:, 2 * dk : 2 * dk + dv],
        qkvs[:, 2 * dk + dv :],
        parts[3].reshape(rank, d).T,
        parts[4].reshape(rank, qk),
        parts[5].reshape(qk),
        parts[2].reshape(dv),
        outs.T,
        parts[1].reshape(d),
        mlp_w[:, :ff],
        mlp_w[:, ff : 2 * ff],
        mlp_w[:, 2 * ff :].T,
    )


def solution(mesh):
    rows, cols = P(("wide", "narrow"), None), P(None, "narrow")
    both = P("wide", "narrow")
    in_specs = (
        rows, rows, P("wide"), P(), cols, cols, cols, cols, P(), P(), P(), P(), P("narrow", None), P(), cols, cols,
        P("narrow", None),
    )
    out_specs = (
        rows, rows, P(), both, both, both, both, P(), P(), P(), P(), P("narrow", "wide"), P(), both, both,
        P("narrow", "wide"),
    )
    return jax.shard_map(shards, mesh=mesh, in_specs=in_specs, out_specs=out_specs, check_vma=False)
```

time: 1690 us -> 535 us (0.32)
  waiting for transfers between devices: 822 us -> 200 us
  matrix products: 241 us -> 18.7 us
  local copies, waits for them, and re-layouts: 253 us -> 70.6 us
  other arithmetic: 207 us -> 55.2 us
  blocking collectives: 124 us -> 0 us
  Pallas kernels: 0 us -> 121 us
  starting transfers between devices: 1.26 us -> 56.6 us
    reduce_scatter x11 -> x0, waiting for transfers between devices: 534 us -> none  [the longest x1 75.6 us: shards(): lax.psum_scatter(grad_mlp_gate, 'wide', scatter_dimension=0, tiled=True)]
    dot_general x44 -> x8, matrix products: 241 us -> 18.7 us  [the longest x5 9.74 us: dot_tn(): lax.dot_general(a, b, (((0,), (0,)), ((), ())), preferred_element_type=F32)]
    psum x2 -> x0, waiting for transfers between devices: 221 us -> none  [the longest x1 123 us: shards(): lax.psum((norm_gain_part, mlp_gain_part, group_part, grad_rank_down, rank...]
    ppermute x0 -> x44, waiting for transfers between devices: none -> 200 us  [hop(): lax.ppermute(value, axis, [(i, i ^ bit) for i in range(lax.axis_size(axis...]
    dynamic_update_slice x161 -> x4, local copies, waits for them, and re-layouts: 153 us -> 0.02 us  [the longest x2 0.02 us: spread(): return lax.dynamic_update_slice_in_dim(zero, other, (place ^ 2) * dk, 1)]
    pallas_call x0 -> x11, Pallas kernels: none -> 121 us  [the longest x4 41 us: mlp(): pl.pallas_call(mlp_kernel, name='mlp', grid=(n // blk,), in_specs=[rows_s...]
    all_gather x3 -> x0, blocking collectives: 85.5 us -> none  [the longest x2 54.1 us: prefix_2(): lax.all_gather(part.astype(kind), axis)]
    mul x120 -> x0, local copies, waits for them, and re-layouts: 82 us -> none  [advance(): return (decay_rate[:, None] * carried + increment, carried)]
  transfers between devices with their start and end apart: 16 -> 44, of which waited for: 13 -> 22; matrix products, arithmetic and copies ran while one was open for 18% -> 16% of each run, Pallas kernels for 0% -> 13%
where the time goes in v1:
time: 535 us; the launch traced here: 525 us
  waiting for transfers between devices  200 us (37%)
  Pallas kernels  121 us (23%)
  local copies, waits for them, and re-layouts  70.6 us (13%)
  starting transfers between devices  56.6 us (11%)
  other arithmetic  55.2 us (10%)
  matrix products  18.7 us (3%)
    ppermute x44, waiting for transfers between devices, hop(): lax.ppermute(value, axis, [(i, i ^ bit) for i in range(lax.axis_size(axis...  200 us
    ppermute x44, starting transfers between devices, hop(): lax.ppermute(value, axis, [(i, i ^ bit) for i in range(lax.axis_size(axis...  56.6 us
    unnamed x198, local copies, waits for them, and re-layouts  47.9 us
    pallas_call x4, Pallas kernels, mlp(): pl.pallas_call(mlp_kernel, name='mlp', grid=(n // blk,), in_specs=[rows_s...  41 us
    pallas_call x2, Pallas kernels, forward_head(): pl.pallas_call(forward_head_kernel, name='forward_head', grid=(n // BLOCK...  25.7 us
    pallas_call x1, Pallas kernels, mlp_grads(): pl.pallas_call(functools.partial(mlp_grads_kernel, pieces), name='mlp_gra...  20.7 us
    pallas_call x2, Pallas kernels, back_head(): pl.pallas_call(back_head_kernel, name='back_head', grid=(n // BLOCK,), in...  18.3 us
  transfers between devices with their start and end apart: 44, of which 22 were waited for; matrix products, arithmetic and copies ran while one was open for 16% of the time, Pallas kernels for 13%

profile of v1, /device:TPU:0, one launch (start us, length us, event | category | flops | bytes accessed | tf_op | source)
XLA Modules:
  0.0 525.4 jit_solution(10267637919294379802)
XLA Ops:
  5.5 2.6 collective-permute-start.1
  8.8 23.1 %collective-permute-done.3 = bf16[128,1024]{1,0:T(8,128)(2,1)S(1)} collective-permute-done((bf16[128,1024]{1,0:T(8,128)(2,1)S(1)}, bf16[128,1024]{1,0:T(8,128)(2,1)S(1)}, u32[]{:S(2)}, u32[]{:S(2)}) %collective-permute-start.3) | collective-permute-done | bytes 262176 | tf_op jit(solution)/shard_map/ppermute | solution.py:385
  34.9 6.1 %collective-permute-done.4 = bf16[128,1024]{1,0:T(8,128)(2,1)S(1)} collective-permute-done((bf16[128,1024]{1,0:T(8,128)(2,1)S(1)}, bf16[128,1024]{1,0:T(8,128)(2,1)S(1)}, u32[]{:S(2)}, u32[]{:S(2)}) %collective-permute-start.4) | collective-permute-done | bytes 262176 | tf_op jit(solution)/shard_map/ppermute | solution.py:385
  41.2 3.9 maximum_select_fusion.x_ref
  45.1 12.8 %forward_head.2 = (bf16[1280,128]{1,0:T(8,128)(2,1)S(1)}, bf16[1280,128]{1,0:T(8,128)(2,1)S(1)}, bf16[1280,256]{1,0:T(8,128)(2,1)S(1)}, f32[1280,256]{1,0:T(8,12...) custom-call(bf16[1280,1024]{1,0:T(8,128)(2,1)} %maximum_select_fusio, ...), custom_call_target="tpu_custom_call" | custom-call | flops 3019898880 | bytes 7741440 | tf_op jit(solution)/shard_map/forward_head/pallas_call | solution.py:128
  59.8 4.2 maximum_select_fusion.2.w_ref
  64.0 12.9 %forward_head.3 = (bf16[1280,128]{1,0:T(8,128)(2,1)S(1)}, bf16[1280,128]{1,0:T(8,128)(2,1)S(1)}, bf16[1280,256]{1,0:T(8,128)(2,1)S(1)}, f32[1280,256]{1,0:T(8,12...) custom-call(bf16[1280,1024]{1,0:T(8,128)(2,1)} %maximum_select_fusio, ...), custom_call_target="tpu_custom_call" | custom-call | flops 3019898880 | bytes 7741440 | tf_op jit(solution)/shard_map/forward_head/pallas_call | solution.py:128
  82.9 1.8 collective-permute-start.5
  84.8 3.3 collective-permute-done.5
  90.0 3.3 collective-permute-done.6
  94.1 1.8 collective-permute-start.7
  96.0 4.3 collective-permute-done.7
  101.1 2.5 collective-permute-start.8
  103.6 3.5 collective-permute-done.8
  108.9 6.8 %gate_out.1 = (f32[1280,256]{1,0:T(8,128)S(1)}, f32[1280,256]{1,0:T(8,128)S(1)}, bf16[1280,256]{1,0:T(8,128)(2,1)S(1)}, bf16[1280,256]{1,0:T(8,128)(2,1)S(1)}, bf16[1280,1024]{1,0:T(8,128)(2,1)}) custom-call(f32[1280,256]{1,0:T(8,128)} %get-tuple-element.88.b0, f32[1280,256]{1,0:T(8,128)} %get-tuple-element.90.b1, ...), custom_call_target="tpu_custom_call" | custom-call | flops 1509949440 | bytes 11796480 | tf_op jit(solution)/shard_map/gate_out/pallas_call | solution.py:173
  119.6 2.6 constant_dynamic-slice_fusion.7
  122.1 3.8 collective-permute-start.13
  126.0 2.4 multiply_reduce_fusion.2
  131.2 3.3 collective-permute-start.12
  135.1 2.6 copy.51.wg_ref
  137.6 2.6 copy.52.wu_ref
  140.3 15.7 %collective-permute-done.13.c_ref.refs_6_ = bf16[640,1024]{1,0:T(8,128)(2,1)} collective-permute-done((bf16[640,1024]{1,0:T(8,128)(2,1)}, bf16[640,1024]{1,0:T(8,128)(2,1)}, u32[]{:S(2)}, u32[]{:S(2)}) %collective-permute-start.13) | collective-permute-done | bytes 1310752 | tf_op jit(solution)/shard_map/ppermute | solution.py:385
  155.9 27.8 %collective-permute-done.12.x_ref.refs_2_ = bf16[640,1024]{1,0:T(8,128)(2,1)} collective-permute-done((bf16[640,1024]{1,0:T(8,128)(2,1)}, bf16[640,1024]{1,0:T(8,128)(2,1)}, u32[]{:S(2)}, u32[]{:S(2)}) %collective-permute-start.12) | collective-permute-done | bytes 1310752 | tf_op jit(solution)/shard_map/ppermute | solution.py:385
  183.8 10.1 %mlp.4 = (bf16[640,704]{1,0:T(8,128)(2,1)S(1)}, bf16[640,704]{1,0:T(8,128)(2,1)S(1)}, bf16[640,704]{1,0:T(8,128)(2,1)S(1)}, bf16[640,1024]{1,0:T(8,128)(2,1)S(1)}, bf16[640,1024]{1,0:T(8,128)(2,1)S(1)}) custom-call(bf16[640,1024]{1,0:T(8,128)(2,1)} %multiply_convert_fusion.x_ref.refs_0_, bf16[640,1024]{1,0:T(8,128)(2,1)} %refs_4_.1, ...), custom_call_target="tpu_custom_call" | custom-call | flops 5536481280 | bytes 12271616 | tf_op jit(solution)/shard_map/mlp/pallas_call | solution.py:207
  195.9 10.6 %mlp.6 = (bf16[640,704]{1,0:T(8,128)(2,1)S(1)}, bf16[640,704]{1,0:T(8,128)(2,1)S(1)}, bf16[640,704]{1,0:T(8,128)(2,1)S(1)}, bf16[640,1024]{1,0:T(8,128)(2,1)S(1)}, bf16[640,1024]{1,0:T(8,128)(2,1)S(1)}) custom-call(bf16[640,1024]{1,0:T(8,128)(2,1)} %collective-permute-done.12.x_ref.refs_2_, bf16[640,1024]{1,0:T(8,128)(2,1)} %collective-permute-done.13.c_ref.refs_6_, ...), custom_call_target="tpu_custom_call" | custom-call | flops 5536481280 | bytes 12271616 | tf_op jit(solution)/shard_map/mlp/pallas_call | solution.py:207
  210.6 10.1 %mlp.5 = (bf16[640,704]{1,0:T(8,128)(2,1)S(1)}, bf16[640,704]{1,0:T(8,128)(2,1)S(1)}, bf16[640,704]{1,0:T(8,128)(2,1)S(1)}, bf16[640,1024]{1,0:T(8,128)(2,1)S(1)}, bf16[640,1024]{1,0:T(8,128)(2,1)S(1)}) custom-call(bf16[640,1024]{1,0:T(8,128)(2,1)} %collective-permute-done.10.x_ref.refs_1_, bf16[640,1024]{1,0:T(8,128)(2,1)} %collective-permute-done.11.c_ref.refs_5_, ...), custom_call_target="tpu_custom_call" | custom-call | flops 5536481280 | bytes 12271616 | tf_op jit(solution)/shard_map/mlp/pallas_call | solution.py:207
  224.0 10.1 %mlp.7 = (bf16[640,704]{1,0:T(8,128)(2,1)S(1)}, bf16[640,704]{1,0:T(8,128)(2,1)S(1)}, bf16[640,704]{1,0:T(8,128)(2,1)S(1)}, bf16[640,1024]{1,0:T(8,128)(2,1)S(1)}, bf16[640,1024]{1,0:T(8,128)(2,1)S(1)}) custom-call(bf16[640,1024]{1,0:T(8,128)(2,1)} %collective-permute-done.14.x_ref.refs_3_, bf16[640,1024]{1,0:T(8,128)(2,1)} %copy-done.92, ...), custom_call_target="tpu_custom_call" | custom-call | flops 5536481280 | bytes 12271616 | tf_op jit(solution)/shard_map/mlp/pallas_call | solution.py:207
  238.3 20.7 %mlp_grads.1 = bf16[1024,2112]{1,0:T(8,128)(2,1)} custom-call(bf16[640,1024]{1,0:T(8,128)(2,1)} %multiply_convert_fusion.x_ref.refs_0_, bf16[640,1024]{1,0:T(8,128)(2,1)} %collective-permute-done.10.x_ref.refs_1_, bf16[640,1024]{1,0:T(8,128)(2,1)} %collective-permute-done.12.x_ref.refs_2_, bf16[640,1024]{1,0:T(8,128)(2,1)} %collective-permute-done.14.x_ref.refs_3_, ...), custom_call_target="tpu_custom_call" | custom-call | flops 11072962560 | bytes 25624576 | tf_op jit(solution)/shard_map/mlp_grads/pallas_call | solution.py:236
  259.0 4.7 constant_dynamic-slice_fusion.1
  263.7 4.2 copy.64
  270.1 2.7 collective-permute-done.17
  272.9 2.9 add_convert_fusion.4
  277.3 4.1 copy.69
  281.4 36.3 %collective-permute-done.41 = bf16[2,2,128,2112]{2,3,0,1:T(8,128)(2,1)} collective-permute-done((bf16[2,2,128,2112]{2,3,0,1:T(8,128)(2,1)}, bf16[2,2,128,2112]{2,3,0,1:T(8,128)(2,1)}, u32[]{:S(2)}, u32[]{:S(2)}) %collective-permute-start.41) | collective-permute-done | bytes 2162720 | tf_op jit(solution)/shard_map/ppermute | solution.py:385
  317.6 3.0 fusion
  321.1 2.9 multiply_reduce_fusion
  324.0 4.8 fusion.28
  328.9 17.4 %collective-permute-done.42 = bf16[2,128,2112]{1,2,0:T(8,128)(2,1)S(1)} collective-permute-done((bf16[2,128,2112]{1,2,0:T(8,128)(2,1)S(1)}, bf16[2,128,2112]{1,2,0:T(8,128)(2,1)S(1)}, u32[]{:S(2)}, u32[]{:S(2)}) %collective-permute-start.42) | collective-permute-done | bytes 1081376 | tf_op jit(solution)/shard_map/ppermute | solution.py:385
  348.4 2.5 maximum_select_fusion.1.gm_ref
  350.9 8.6 %gate_back.1 = (bf16[1280,256]{1,0:T(8,128)(2,1)S(1)}, bf16[1280,256]{1,0:T(8,128)(2,1)S(1)}, bf16[1280,256]{1,0:T(8,128)(2,1)S(1)}, bf16[1280,256]{1,0:T(8,128)...) custom-call(bf16[1280,1024]{1,0:T(8,128)(2,1)} %maximum_select_fusion.1.gm_ref, ...), custom_call_target="tpu_custom_call" | custom-call | flops 1509949440 | bytes 11796480 | tf_op jit(solution)/shard_map/gate_back/pallas_call | solution.py:282
  364.6 7.6 %collective-permute-done.43 = bf16[128,2112]{0,1:T(8,128)(2,1)S(1)} collective-permute-done((bf16[128,2112]{0,1:T(8,128)(2,1)S(1)}, bf16[128,2112]{0,1:T(8,128)(2,1)S(1)}, u32[]{:S(2)}, u32[]{:S(2)}) %collective-permute-start.43) | collective-permute-done | bytes 540704 | tf_op jit(solution)/shard_map/ppermute | solution.py:385
  376.8 2.3 collective-permute-done.24
  382.1 2.3 collective-permute-done.25
  387.2 6.1 %collective-permute-done.37 = bf16[1024,256]{1,0:T(8,128)(2,1)S(1)} collective-permute-done((bf16[1024,256]{1,0:T(8,128)(2,1)S(1)}, bf16[1024,256]{1,0:T(8,128)(2,1)S(1)}, u32[]{:S(2)}, u32[]{:S(2)}) %collective-permute-start.37) | collective-permute-done | bytes 524320 | tf_op jit(solution)/shard_map/ppermute | solution.py:385
  395.1 1.8 copy.62
  406.0 9.0 %back_head.3 = (bf16[1280,768]{1,0:T(8,128)(2,1)}, f32[1280,16]{1,0:T(8,128)S(1)}, f32[16,128]{1,0:T(8,128)S(1)}, f32[1,128]{1,0:T(1,128)S(1)}) custom-call(bf16[1280,128]{1,0:T(8,128)(2,1)S(1)} %copy-done.42, bf16[1280,128]{1,0:T(8,128)(2,1)S(1)} %copy-done.44, bf16[1280,256]{1,0:T(8,128)(2,1)S(1)} %copy-done.22, f32[1280,128]{1,0:T(8,128)S(1)} %copy-done.24, ...), custom_call_target="tpu_custom_call" | custom-call | flops 838860800 | bytes 7680000 | tf_op jit(solution)/shard_map/back_head/pallas_call | solution.py:367
  415.0 3.9 fusion.36
  419.0 3.5 convolution_convert_fusion
  422.6 9.3 %back_head.2 = (bf16[1280,768]{1,0:T(8,128)(2,1)}, f32[1280,16]{1,0:T(8,128)S(1)}, f32[16,128]{1,0:T(8,128)S(1)}, f32[1,128]{1,0:T(1,128)S(1)}) custom-call(bf16[1280,128]{1,0:T(8,128)(2,1)S(1)} %copy-done.38, bf16[1280,128]{1,0:T(8,128)(2,1)S(1)} %copy-done.40, bf16[1280,256]{1,0:T(8,128)(2,1)S(1)} %copy-done.14, f32[1280,128]{1,0:T(8,128)S(1)} %copy-done.16, ...), custom_call_target="tpu_custom_call" | custom-call | flops 838860800 | bytes 7680000 | tf_op jit(solution)/shard_map/back_head/pallas_call | solution.py:367
  431.9 4.2 fusion.35
  443.2 3.9 collective-permute-done.39
  447.1 2.9 collective-permute-start.40
  450.0 3.1 fusion.10
  455.5 3.0 add_convert_fusion.3
  459.9 18.1 %collective-permute-done.29 = f32[214,128]{1,0:T(8,128)S(1)} collective-permute-done((f32[214,128]{1,0:T(8,128)S(1)}, f32[214,128]{1,0:T(8,128)S(1)}, u32[]{:S(2)}, u32[]{:S(2)}) %collective-permute-start.29) | collective-permute-done | bytes 109600 | tf_op jit(solution)/shard_map/ppermute | solution.py:385
  478.4 3.9 add_convert_fusion.1
  487.0 3.0 collective-permute-done.31
  490.0 2.9 collective-permute-start.32
  493.0 3.7 fusion.9
  498.6 3.6 collective-permute-done.34
  507.5 6.3 %collective-permute-done.35 = bf16[2,128,768]{2,1,0:T(8,128)(2,1)S(1)} collective-permute-done((bf16[2,128,768]{2,1,0:T(8,128)(2,1)S(1)}, bf16[2,128,768]{2,1,0:T(8,128)(2,1)S(1)}, u32[]{:S(2)}, u32[]{:S(2)}) %collective-permute-start.35) | collective-permute-done | bytes 393248 | tf_op jit(solution)/shard_map/ppermute | solution.py:385
  514.0 3.5 collective-permute-start.36
  517.4 3.3 add_convert_fusion.2
  520.8 2.8 collective-permute-done.36
  (369 shorter events, 98.6 us)
Async XLA Ops:
  4.6 36.6 %collective-permute-start = (bf16[640,1024]{1,0:T(8,128)(2,1)}, bf16[640,1024]{1,0:T(8,128)(2,1)}, u32[]{:S(2)}, u32[]{:S(2)}) collective-permute-start(bf16[640,1024]{1,0:T(8,128)(2,1)} %fusion.5), channel_id=1, source_target_pairs={{0,1},{1,0},{2,3},{3,2},{4,5},{5,4},{6,7},{7,6},{8,9},{9,8},{10,11... | collective-permute-start | bytes 3932168 | tf_op jit(solution)/shard_map/ppermute | solution.py:385
  5.2 28.4 %copy-start.85 = (bf16[1024,16]{0,1:T(8,128)(2,1)S(1)}, bf16[1024,16]{0,1:T(8,128)(2,1)}, u32[]{:S(2)}) copy-start(bf16[1024,16]{0,1:T(8,128)(2,1)} %param.25) | copy-start | bytes 98308
  5.3 29.2 %copy-start.89 = (bf16[512]{0:T(512)(128)(2,1)S(1)}, bf16[512]{0:T(512)(128)(2,1)}, u32[]{:S(2)}) copy-start(bf16[512]{0:T(512)(128)(2,1)} %param.27) | copy-start | bytes 3076
  5.3 29.3 %copy-start.87 = (bf16[16,512]{1,0:T(8,128)(2,1)S(1)}, bf16[16,512]{1,0:T(8,128)(2,1)}, u32[]{:S(2)}) copy-start(bf16[16,512]{1,0:T(8,128)(2,1)} %param.26) | copy-start | bytes 49156
  5.4 28.2 %copy-start.80 = (bf16[1024,768]{1,0:T(8,128)(2,1)}, bf16[1024,768]{1,0:T(8,128)(2,1)S(1)}, u32[]{:S(2)}) copy-start(bf16[1024,768]{1,0:T(8,128)(2,1)S(1)} %constant_dynamic-update-slice_fusion.w_ref) | copy-start | bytes 4718596
  5.5 29.1 %collective-permute-start.1 = (bf16[512,768]{1,0:T(8,128)(2,1)S(1)}, bf16[512,768]{1,0:T(8,128)(2,1)}, u32[]{:S(2)}, u32[]{:S(2)}) collective-permute-start(bf16[512,768]{1,0:T(8,128)(2,1)S(1)} %constant_dynamic-slice_fusion.10), channel_id=1, source_target_pairs={{0,2},{1,3},{2,0},{3,1},{4,6},{5,7},{6,4},{7,5},{8,10},{9,11},{10,... | collective-permute-start | bytes 2359304 | tf_op jit(solution)/shard_map/ppermute | solution.py:385
  8.1 23.8 %collective-permute-start.3 = (bf16[128,1024]{1,0:T(8,128)(2,1)S(1)}, bf16[128,1024]{1,0:T(8,128)(2,1)S(1)}, u32[]{:S(2)}, u32[]{:S(2)}) collective-permute-start(bf16[128,1024]{1,0:T(8,128)(2,1)S(1)} %constant_dynamic-slice_fusion.9), channel_id=1, source_target_pairs={{0,2},{1,3},{2,0},{3,1},{4,6},{5,7},{6,4},{7,5},{8,10},{9,11},{10,... | collective-permute-start | bytes 786440 | tf_op jit(solution)/shard_map/ppermute | solution.py:385
  31.9 9.2 %collective-permute-start.4 = (bf16[128,1024]{1,0:T(8,128)(2,1)S(1)}, bf16[128,1024]{1,0:T(8,128)(2,1)S(1)}, u32[]{:S(2)}, u32[]{:S(2)}) collective-permute-start(bf16[128,1024]{1,0:T(8,128)(2,1)S(1)} %collective-permute-done.3), channel_id=1, source_target_pairs={{0,4},{4,0},{8,12},{12,8},{16,20},{20,16},{24,28},{28,24},{1,5},{5... | collective-permute-start | bytes 786440 | tf_op jit(solution)/shard_map/ppermute | solution.py:385
  34.6 25.2 %collective-permute-start.2 = (bf16[512,768]{1,0:T(8,128)(2,1)}, bf16[512,768]{1,0:T(8,128)(2,1)S(1)}, u32[]{:S(2)}, u32[]{:S(2)}) collective-permute-start(bf16[512,768]{1,0:T(8,128)(2,1)} %collective-permute-done.1), channel_id=1, source_target_pairs={{0,4},{4,0},{8,12},{12,8},{16,20},{20,16},{24,28},{28,24},{1,5},{5... | collective-permute-start | bytes 2359304 | tf_op jit(solution)/shard_map/ppermute | solution.py:385
  82.9 26.0 %copy-start.6 = (bf16[1280,128]{1,0:T(8,128)(2,1)}, bf16[1280,128]{1,0:T(8,128)(2,1)S(1)}, u32[]{:S(2)}) copy-start(bf16[1280,128]{1,0:T(8,128)(2,1)S(1)} %get-tuple-element.92.r1) | copy-start | bytes 983044
  82.9 5.1 collective-permute-start.5
  88.1 15.5 %copy-start.93 = (bf16[256]{0:T(256)(128)(2,1)S(1)}, bf16[256]{0:T(256)(128)(2,1)}, u32[]{:S(2)}) copy-start(bf16[256]{0:T(256)(128)(2,1)} %param.28) | copy-start | bytes 1540
  88.2 5.1 collective-permute-start.6
  94.1 6.2 %collective-permute-start.7 = (bf16[2,272,128]{2,1,0:T(8,128)(2,1)}, bf16[2,272,128]{2,1,0:T(8,128)(2,1)S(1)}, u32[]{:S(2)}, u32[]{:S(2)}) collective-permute-start(bf16[2,272,128]{2,1,0:T(8,128)(2,1)} %pad_maximum_fusion.4), channel_id=1, source_target_pairs={{0,8},{4,12},{8,0},{12,4},{16,24},{20,28},{24,16},{28,20},{1,9},{5... | collective-permute-start | bytes 417800 | tf_op jit(solution)/shard_map/ppermute | solution.py:385
  101.1 6.0 %collective-permute-start.8 = (bf16[2,272,128]{2,1,0:T(8,128)(2,1)S(1)}, bf16[2,272,128]{2,1,0:T(8,128)(2,1)S(1)}, u32[]{:S(2)}, u32[]{:S(2)}) collective-permute-start(bf16[2,272,128]{2,1,0:T(8,128)(2,1)S(1)} %pad_maximum_fusion.5), channel_id=1, source_target_pairs={{0,16},{4,20},{8,24},{12,28},{16,0},{20,4},{24,8},{28,12},{1,17},{... | collective-permute-start | bytes 417800 | tf_op jit(solution)/shard_map/ppermute | solution.py:385
  122.1 3.8 collective-permute-start.9
  122.1 33.8 %collective-permute-start.13 = (bf16[640,1024]{1,0:T(8,128)(2,1)}, bf16[640,1024]{1,0:T(8,128)(2,1)}, u32[]{:S(2)}, u32[]{:S(2)}) collective-permute-start(bf16[640,1024]{1,0:T(8,128)(2,1)} %refs_4_.1), channel_id=1, source_target_pairs={{0,2},{1,3},{2,0},{3,1},{4,6},{5,7},{6,4},{7,5},{8,10},{9,11},{10,... | collective-permute-start | bytes 3932168 | tf_op jit(solution)/shard_map/ppermute | solution.py:385
  131.2 52.5 %collective-permute-start.12 = (bf16[640,1024]{1,0:T(8,128)(2,1)}, bf16[640,1024]{1,0:T(8,128)(2,1)}, u32[]{:S(2)}, u32[]{:S(2)}) collective-permute-start(bf16[640,1024]{1,0:T(8,128)(2,1)} %multiply_convert_fusion.x_ref.refs_0_), channel_id=1, source_target_pairs={{0,2},{1,3},{2,0},{3,1},{4,6},{5,7},{6,4},{7,5},{8,10},{9,11},{10,... | collective-permute-start | bytes 3932168 | tf_op jit(solution)/shard_map/ppermute | solution.py:385
  134.5 76.0 %collective-permute-start.11 = (bf16[640,1024]{1,0:T(8,128)(2,1)}, bf16[640,1024]{1,0:T(8,128)(2,1)}, u32[]{:S(2)}, u32[]{:S(2)}) collective-permute-start(bf16[640,1024]{1,0:T(8,128)(2,1)} %refs_4_.1), channel_id=1, source_target_pairs={{0,1},{1,0},{2,3},{3,2},{4,5},{5,4},{6,7},{7,6},{8,9},{9,8},{10,11... | collective-permute-start | bytes 3932168 | tf_op jit(solution)/shard_map/ppermute | solution.py:385
  134.5 76.0 %collective-permute-start.10 = (bf16[640,1024]{1,0:T(8,128)(2,1)}, bf16[640,1024]{1,0:T(8,128)(2,1)}, u32[]{:S(2)}, u32[]{:S(2)}) collective-permute-start(bf16[640,1024]{1,0:T(8,128)(2,1)} %multiply_convert_fusion.x_ref.refs_0_), channel_id=1, source_target_pairs={{0,1},{1,0},{2,3},{3,2},{4,5},{5,4},{6,7},{7,6},{8,9},{9,8},{10,11... | collective-permute-start | bytes 3932168 | tf_op jit(solution)/shard_map/ppermute | solution.py:385
  155.9 65.9 %collective-permute-start.15 = (bf16[640,1024]{1,0:T(8,128)(2,1)}, bf16[640,1024]{1,0:T(8,128)(2,1)S(1)}, u32[]{:S(2)}, u32[]{:S(2)}) collective-permute-start(bf16[640,1024]{1,0:T(8,128)(2,1)} %collective-permute-done.13.c_ref.refs_6_), channel_id=1, source_target_pairs={{0,1},{1,0},{2,3},{3,2},{4,5},{5,4},{6,7},{7,6},{8,9},{9,8},{10,11... | collective-permute-start | bytes 3932168 | tf_op jit(solution)/shard_map/ppermute | solution.py:385
  183.8 39.2 %collective-permute-start.14 = (bf16[640,1024]{1,0:T(8,128)(2,1)}, bf16[640,1024]{1,0:T(8,128)(2,1)}, u32[]{:S(2)}, u32[]{:S(2)}) collective-permute-start(bf16[640,1024]{1,0:T(8,128)(2,1)} %collective-permute-done.12.x_ref.refs_2_), channel_id=1, source_target_pairs={{0,1},{1,0},{2,3},{3,2},{4,5},{5,4},{6,7},{7,6},{8,9},{9,8},{10,11... | collective-permute-start | bytes 3932168 | tf_op jit(solution)/shard_map/ppermute | solution.py:385
  221.8 12.3 %copy-start.56 = (bf16[640,704]{1,0:T(8,128)(2,1)}, bf16[640,704]{1,0:T(8,128)(2,1)S(1)}, u32[]{:S(2)}) copy-start(bf16[640,704]{1,0:T(8,128)(2,1)S(1)} %get-tuple-element.157.refs_17_) | copy-start | bytes 2703364
  267.9 49.8 %collective-permute-start.41 = (bf16[2,2,128,2112]{2,3,0,1:T(8,128)(2,1)}, bf16[2,2,128,2112]{2,3,0,1:T(8,128)(2,1)}, u32[]{:S(2)}, u32[]{:S(2)}) collective-permute-start(bf16[2,2,128,2112]{2,3,0,1:T(8,128)(2,1)} %bitcast.150), channel_id=1, source_target_pairs={{0,4},{4,0},{8,12},{12,8},{16,20},{20,16},{24,28},{28,24},{1,5},{5... | collective-permute-start | bytes 6488072 | tf_op jit(solution)/shard_map/ppermute | solution.py:385
  269.6 3.2 collective-permute-start.17
  269.8 51.3 %collective-permute-start.16 = (bf16[640,1024]{1,0:T(8,128)(2,1)}, bf16[640,1024]{1,0:T(8,128)(2,1)}, u32[]{:S(2)}, u32[]{:S(2)}) collective-permute-start(bf16[640,1024]{1,0:T(8,128)(2,1)} %copy-done.47), channel_id=1, source_target_pairs={{0,1},{1,0},{2,3},{3,2},{4,5},{5,4},{6,7},{7,6},{8,9},{9,8},{10,11... | collective-permute-start | bytes 3932168 | tf_op jit(solution)/shard_map/ppermute | solution.py:385
  275.8 45.4 %collective-permute-start.18 = (bf16[640,1024]{1,0:T(8,128)(2,1)}, bf16[640,1024]{1,0:T(8,128)(2,1)}, u32[]{:S(2)}, u32[]{:S(2)}) collective-permute-start(bf16[640,1024]{1,0:T(8,128)(2,1)} %add_convert_fusion.4), channel_id=1, source_target_pairs={{0,2},{1,3},{2,0},{3,1},{4,6},{5,7},{6,4},{7,5},{8,10},{9,11},{10,... | collective-permute-start | bytes 3932168 | tf_op jit(solution)/shard_map/ppermute | solution.py:385
  320.7 25.6 %collective-permute-start.42 = (bf16[2,128,2112]{1,2,0:T(8,128)(2,1)S(1)}, bf16[2,128,2112]{1,2,0:T(8,128)(2,1)S(1)}, u32[]{:S(2)}, u32[]{:S(2)}) collective-permute-start(bf16[2,128,2112]{1,2,0:T(8,128)(2,1)S(1)} %dynamic-slice_bitcast_fusion), channel_id=1, source_target_pairs={{0,8},{4,12},{8,0},{12,4},{16,24},{20,28},{24,16},{28,20},{1,9},{5... | collective-permute-start | bytes 3244040 | tf_op jit(solution)/shard_map/ppermute | solution.py:385
  328.9 19.5 %collective-permute-start.19 = (bf16[640,1024]{1,0:T(8,128)(2,1)S(1)}, bf16[640,1024]{1,0:T(8,128)(2,1)S(1)}, u32[]{:S(2)}, u32[]{:S(2)}) collective-permute-start(bf16[640,1024]{1,0:T(8,128)(2,1)S(1)} %get-tuple-element.169), channel_id=1, source_target_pairs={{0,1},{1,0},{2,3},{3,2},{4,5},{5,4},{6,7},{7,6},{8,9},{9,8},{10,11... | collective-permute-start | bytes 3932168 | tf_op jit(solution)/shard_map/ppermute | solution.py:385
  346.6 25.6 %collective-permute-start.43 = (bf16[128,2112]{0,1:T(8,128)(2,1)S(1)}, bf16[128,2112]{0,1:T(8,128)(2,1)S(1)}, u32[]{:S(2)}, u32[]{:S(2)}) collective-permute-start(bf16[128,2112]{0,1:T(8,128)(2,1)S(1)} %dynamic-slice_bitcast_fusion.1), channel_id=1, source_target_pairs={{0,16},{4,20},{8,24},{12,28},{16,0},{20,4},{24,8},{28,12},{1,17},{... | collective-permute-start | bytes 1622024 | tf_op jit(solution)/shard_map/ppermute | solution.py:385
  363.0 10.2 %collective-permute-start.23 = (bf16[2,272,128]{2,1,0:T(8,128)(2,1)S(1)}, bf16[2,272,128]{2,1,0:T(8,128)(2,1)S(1)}, u32[]{:S(2)}, u32[]{:S(2)}) collective-permute-start(bf16[2,272,128]{2,1,0:T(8,128)(2,1)S(1)} %pad_maximum_fusion.1), channel_id=1, source_target_pairs={{0,2},{1,3},{2,0},{3,1},{4,6},{5,7},{6,4},{7,5},{8,10},{9,11},{10,... | collective-permute-start | bytes 417800 | tf_op jit(solution)/shard_map/ppermute | solution.py:385
  373.5 5.6 %collective-permute-start.24 = (bf16[2,272,128]{2,1,0:T(8,128)(2,1)S(1)}, bf16[2,272,128]{2,1,0:T(8,128)(2,1)S(1)}, u32[]{:S(2)}, u32[]{:S(2)}) collective-permute-start(bf16[2,272,128]{2,1,0:T(8,128)(2,1)S(1)} %pad_maximum_fusion.6), channel_id=1, source_target_pairs={{0,4},{4,0},{8,12},{12,8},{16,20},{20,16},{24,28},{28,24},{1,5},{5... | collective-permute-start | bytes 417800 | tf_op jit(solution)/shard_map/ppermute | solution.py:385
  376.3 79.3 %collective-permute-start.21 = (bf16[640,1024]{1,0:T(8,128)(2,1)}, bf16[640,1024]{1,0:T(8,128)(2,1)}, u32[]{:S(2)}, u32[]{:S(2)}) collective-permute-start(bf16[640,1024]{1,0:T(8,128)(2,1)} %copy-done.46), channel_id=1, source_target_pairs={{0,1},{1,0},{2,3},{3,2},{4,5},{5,4},{6,7},{7,6},{8,9},{9,8},{10,11... | collective-permute-start | bytes 3932168 | tf_op jit(solution)/shard_map/ppermute | solution.py:385
  376.3 141.2 %collective-permute-start.20 = (bf16[640,1024]{1,0:T(8,128)(2,1)}, bf16[640,1024]{1,0:T(8,128)(2,1)}, u32[]{:S(2)}, u32[]{:S(2)}) collective-permute-start(bf16[640,1024]{1,0:T(8,128)(2,1)} %copy-done.45), channel_id=1, source_target_pairs={{0,1},{1,0},{2,3},{3,2},{4,5},{5,4},{6,7},{7,6},{8,9},{9,8},{10,11... | collective-permute-start | bytes 3932168 | tf_op jit(solution)/shard_map/ppermute | solution.py:385
  379.3 5.1 collective-permute-start.25
  379.4 13.9 %copy-start.50 = (bf16[1280,256]{1,0:T(8,128)(2,1)S(1)}, bf16[1280,256]{1,0:T(8,128)(2,1)}, u32[]{:S(2)}) copy-start(bf16[1280,256]{1,0:T(8,128)(2,1)} %copy-done.49) | copy-start | bytes 1966084
  380.3 13.0 %collective-permute-start.37 = (bf16[1024,256]{1,0:T(8,128)(2,1)S(1)}, bf16[1024,256]{1,0:T(8,128)(2,1)S(1)}, u32[]{:S(2)}, u32[]{:S(2)}) collective-permute-start(bf16[1024,256]{1,0:T(8,128)(2,1)S(1)} %convolution_convert_fusion.1), channel_id=1, source_target_pairs={{0,2},{1,3},{2,0},{3,1},{4,6},{5,7},{6,4},{7,5},{8,10},{9,11},{10,... | collective-permute-start | bytes 1572872 | tf_op jit(solution)/shard_map/ppermute | solution.py:385
  385.8 14.7 %collective-permute-start.26 = (bf16[2,272,128]{2,1,0:T(8,128)(2,1)}, bf16[2,272,128]{2,1,0:T(8,128)(2,1)S(1)}, u32[]{:S(2)}, u32[]{:S(2)}) collective-permute-start(bf16[2,272,128]{2,1,0:T(8,128)(2,1)} %pad_maximum_fusion.8), channel_id=1, source_target_pairs={{0,16},{4,20},{8,24},{12,28},{16,0},{20,4},{24,8},{28,12},{1,17},{... | collective-permute-start | bytes 417800 | tf_op jit(solution)/shard_map/ppermute | solution.py:385
  394.2 7.5 %copy-start.22 = (bf16[1280,256]{1,0:T(8,128)(2,1)S(1)}, bf16[1280,256]{1,0:T(8,128)(2,1)}, u32[]{:S(2)}) copy-start(bf16[1280,256]{1,0:T(8,128)(2,1)} %copy-done.21) | copy-start | bytes 1966084
  394.3 7.5 %copy-start.24 = (f32[1280,128]{1,0:T(8,128)S(1)}, f32[1280,128]{1,0:T(8,128)}, u32[]{:S(2)}) copy-start(f32[1280,128]{1,0:T(8,128)} %copy-done.23) | copy-start | bytes 1966084
  394.3 7.5 %copy-start.26 = (f32[1280,128]{1,0:T(8,128)S(1)}, f32[1280,128]{1,0:T(8,128)}, u32[]{:S(2)}) copy-start(f32[1280,128]{1,0:T(8,128)} %copy-done.25) | copy-start | bytes 1966084
  397.0 43.3 %collective-permute-start.38 = (bf16[2,2,128,256]{2,3,0,1:T(8,128)(2,1)}, bf16[2,2,128,256]{2,3,0,1:T(8,128)(2,1)}, u32[]{:S(2)}, u32[]{:S(2)}) collective-permute-start(bf16[2,2,128,256]{2,3,0,1:T(8,128)(2,1)} %bitcast.153), channel_id=1, source_target_pairs={{0,4},{4,0},{8,12},{12,8},{16,20},{20,16},{24,28},{28,24},{1,5},{5... | collective-permute-start | bytes 786440 | tf_op jit(solution)/shard_map/ppermute | solution.py:385
  406.0 9.0 %copy-start.76 = (bf16[1024,768]{1,0:T(8,128)(2,1)S(1)}, bf16[1024,768]{1,0:T(8,128)(2,1)}, u32[]{:S(2)}) copy-start(bf16[1024,768]{1,0:T(8,128)(2,1)} %maximum_select_fusion.2.w_ref) | copy-start | bytes 4718596
  438.3 11.7 %collective-permute-start.27 = (bf16[640,1024]{1,0:T(8,128)(2,1)}, bf16[640,1024]{1,0:T(8,128)(2,1)}, u32[]{:S(2)}, u32[]{:S(2)}) collective-permute-start(bf16[640,1024]{1,0:T(8,128)(2,1)} %constant_dynamic-slice_fusion.6), channel_id=1, source_target_pairs={{0,1},{1,0},{2,3},{3,2},{4,5},{5,4},{6,7},{7,6},{8,9},{9,8},{10,11... | collective-permute-start | bytes 3932168 | tf_op jit(solution)/shard_map/ppermute | solution.py:385
  438.3 40.2 %collective-permute-start.33 = (bf16[1024,768]{1,0:T(8,128)(2,1)}, bf16[1024,768]{1,0:T(8,128)(2,1)}, u32[]{:S(2)}, u32[]{:S(2)}) collective-permute-start(bf16[1024,768]{1,0:T(8,128)(2,1)} %convolution_convert_fusion), channel_id=1, source_target_pairs={{0,2},{1,3},{2,0},{3,1},{4,6},{5,7},{6,4},{7,5},{8,10},{9,11},{10,... | collective-permute-start | bytes 4718600 | tf_op jit(solution)/shard_map/ppermute | solution.py:385
  441.4 5.7 %collective-permute-start.39 = (bf16[2,128,256]{1,2,0:T(8,128)(2,1)S(1)}, bf16[2,128,256]{1,2,0:T(8,128)(2,1)S(1)}, u32[]{:S(2)}, u32[]{:S(2)}) collective-permute-start(bf16[2,128,256]{1,2,0:T(8,128)(2,1)S(1)} %dynamic-slice_bitcast_fusion.4), channel_id=1, source_target_pairs={{0,8},{4,12},{8,0},{12,4},{16,24},{20,28},{24,16},{28,20},{1,9},{5... | collective-permute-start | bytes 393224 | tf_op jit(solution)/shard_map/ppermute | solution.py:385
  447.1 8.4 %copy-start.9 = (bf16[640,1024]{1,0:T(8,128)(2,1)S(1)}, bf16[640,1024]{1,0:T(8,128)(2,1)}, u32[]{:S(2)}) copy-start(bf16[640,1024]{1,0:T(8,128)(2,1)} %copy-done.8) | copy-start | bytes 3932164
  447.1 6.5 %collective-permute-start.40 = (bf16[128,256]{0,1:T(8,128)(2,1)S(1)}, bf16[128,256]{0,1:T(8,128)(2,1)S(1)}, u32[]{:S(2)}, u32[]{:S(2)}) collective-permute-start(bf16[128,256]{0,1:T(8,128)(2,1)S(1)} %dynamic-slice_bitcast_fusion.5), channel_id=1, source_target_pairs={{0,16},{4,20},{8,24},{12,28},{16,0},{20,4},{24,8},{28,12},{1,17},{... | collective-permute-start | bytes 196616 | tf_op jit(solution)/shard_map/ppermute | solution.py:385
  453.5 1.4 collective-permute-start.28
  454.3 24.1 %copy-start.68 = (bf16[1280,1024]{1,0:T(8,128)(2,1)S(1)}, bf16[1280,1024]{1,0:T(8,128)(2,1)}, u32[]{:S(2)}) copy-start(bf16[1280,1024]{1,0:T(8,128)(2,1)} %maximum_select_fusion.x_ref) | copy-start | bytes 7864324
  454.3 24.1 %copy-start.90 = (bf16[1280,768]{1,0:T(8,128)(2,1)S(1)}, bf16[1280,768]{1,0:T(8,128)(2,1)}, u32[]{:S(2)}) copy-start(bf16[1280,768]{1,0:T(8,128)(2,1)} %get-tuple-element.128) | copy-start | bytes 5898244
  454.9 23.1 %collective-permute-start.29 = (f32[214,128]{1,0:T(8,128)S(1)}, f32[214,128]{1,0:T(8,128)S(1)}, u32[]{:S(2)}, u32[]{:S(2)}) collective-permute-start(f32[214,128]{1,0:T(8,128)S(1)} %add.260), channel_id=1, source_target_pairs={{0,2},{1,3},{2,0},{3,1},{4,6},{5,7},{6,4},{7,5},{8,10},{9,11},{10,... | collective-permute-start | bytes 328712 | tf_op jit(solution)/shard_map/ppermute | solution.py:385
  458.6 58.8 %collective-permute-start.22 = (bf16[640,1024]{1,0:T(8,128)(2,1)}, bf16[640,1024]{1,0:T(8,128)(2,1)S(1)}, u32[]{:S(2)}, u32[]{:S(2)}) collective-permute-start(bf16[640,1024]{1,0:T(8,128)(2,1)} %add_convert_fusion.3), channel_id=1, source_target_pairs={{0,2},{1,3},{2,0},{3,1},{4,6},{5,7},{6,4},{7,5},{8,10},{9,11},{10,... | collective-permute-start | bytes 3932168 | tf_op jit(solution)/shard_map/ppermute | solution.py:385
  478.1 7.1 %collective-permute-start.30 = (f32[214,128]{1,0:T(8,128)S(1)}, f32[214,128]{1,0:T(8,128)S(1)}, u32[]{:S(2)}, u32[]{:S(2)}) collective-permute-start(f32[214,128]{1,0:T(8,128)S(1)} %add.261), channel_id=1, source_target_pairs={{0,4},{4,0},{8,12},{12,8},{16,20},{20,16},{24,28},{28,24},{1,5},{5... | collective-permute-start | bytes 328712 | tf_op jit(solution)/shard_map/ppermute | solution.py:385
  478.4 14.5 %copy-start.69 = (f32[640,1024]{1,0:T(8,128)S(1)}, f32[640,1024]{1,0:T(8,128)}, u32[]{:S(2)}) copy-start(f32[640,1024]{1,0:T(8,128)} %get-tuple-element.170) | copy-start | bytes 7864324
  482.4 10.6 %copy-start.64 = (bf16[640,1024]{1,0:T(8,128)(2,1)S(1)}, bf16[640,1024]{1,0:T(8,128)(2,1)}, u32[]{:S(2)}) copy-start(bf16[640,1024]{1,0:T(8,128)(2,1)} %param.17) | copy-start | bytes 3932164
  482.4 10.5 %copy-start.66 = (bf16[1280,1024]{1,0:T(8,128)(2,1)S(1)}, bf16[1280,1024]{1,0:T(8,128)(2,1)}, u32[]{:S(2)}) copy-start(bf16[1280,1024]{1,0:T(8,128)(2,1)} %copy-done.65) | copy-start | bytes 7864324
  483.5 18.7 %collective-permute-start.34 = (bf16[2,2,128,768]{3,2,0,1:T(8,128)(2,1)}, bf16[2,2,128,768]{3,2,0,1:T(8,128)(2,1)S(1)}, u32[]{:S(2)}, u32[]{:S(2)}) collective-permute-start(bf16[2,2,128,768]{3,2,0,1:T(8,128)(2,1)} %bitcast.127), channel_id=1, source_target_pairs={{0,4},{4,0},{8,12},{12,8},{16,20},{20,16},{24,28},{28,24},{1,5},{5... | collective-permute-start | bytes 2359304 | tf_op jit(solution)/shard_map/ppermute | solution.py:385
  485.2 4.8 collective-permute-start.31
  490.0 6.6 %collective-permute-start.32 = (f32[214,128]{1,0:T(8,128)S(1)}, f32[214,128]{1,0:T(8,128)S(1)}, u32[]{:S(2)}, u32[]{:S(2)}) collective-permute-start(f32[214,128]{1,0:T(8,128)S(1)} %add.263), channel_id=1, source_target_pairs={{0,16},{4,20},{8,24},{12,28},{16,0},{20,4},{24,8},{28,12},{1,17},{... | collective-permute-start | bytes 328712 | tf_op jit(solution)/shard_map/ppermute | solution.py:385
  503.1 14.4 %copy-start.12 = (bf16[640,1024]{1,0:T(8,128)(2,1)S(1)}, bf16[640,1024]{1,0:T(8,128)(2,1)}, u32[]{:S(2)}) copy-start(bf16[640,1024]{1,0:T(8,128)(2,1)} %copy-done.11) | copy-start | bytes 3932164
  503.1 14.4 %copy-start.61 = (f32[640,1024]{1,0:T(8,128)S(1)}, f32[640,1024]{1,0:T(8,128)}, u32[]{:S(2)}) copy-start(f32[640,1024]{1,0:T(8,128)} %copy-done.59) | copy-start | bytes 7864324
  504.6 9.2 %collective-permute-start.35 = (bf16[2,128,768]{2,1,0:T(8,128)(2,1)S(1)}, bf16[2,128,768]{2,1,0:T(8,128)(2,1)S(1)}, u32[]{:S(2)}, u32[]{:S(2)}) collective-permute-start(bf16[2,128,768]{2,1,0:T(8,128)(2,1)S(1)} %dynamic-slice_bitcast_fusion.2), channel_id=1, source_target_pairs={{0,8},{4,12},{8,0},{12,4},{16,24},{20,28},{24,16},{28,20},{1,9},{5... | collective-permute-start | bytes 1179656 | tf_op jit(solution)/shard_map/ppermute | solution.py:385
  514.0 9.6 %collective-permute-start.36 = (bf16[128,768]{1,0:T(8,128)(2,1)S(1)}, bf16[128,768]{1,0:T(8,128)(2,1)S(1)}, u32[]{:S(2)}, u32[]{:S(2)}) collective-permute-start(bf16[128,768]{1,0:T(8,128)(2,1)S(1)} %dynamic-slice_bitcast_fusion.3), channel_id=1, source_target_pairs={{0,16},{4,20},{8,24},{12,28},{16,0},{20,4},{24,8},{28,12},{1,17},{... | collective-permute-start | bytes 589832 | tf_op jit(solution)/shard_map/ppermute | solution.py:385
  (74 other events, 180.8 us)
